TPU v7x, 256 devices: a whole 4x4x8 slice. The times are simulated.
256 devices in a mesh: row: 32 (over x_hi, z, core), col: 8 (over y, x_lo).
Axes of the slice: x: 4 (x_hi: 2, x_lo: 2; x = x_hi * 2 + x_lo), y: 4, z: 8, core: 2. Of those that a mesh axis runs over, the one named last changes fastest.
Arguments:
- p_tiles: bfloat16 [1024, 2, 128, 128], P(('row', 'col')), may hold values from -0.5 to 0.5
- p_cols: int32 [1024, 2], P(('row', 'col')), may hold values from 0 to 31, as said below
- q_tiles: bfloat16 [1024, 6, 128, 128], P(('row', 'col')), may hold values from -1.796875 to 1.796875
- q_cols: int32 [1024, 6], P(('row', 'col')), may hold values from 0 to 31, all different within a row
Outputs:
- coarse: float32 [4096, 4096], P('row', 'col')
Inputs may be any that keep to these rules, and one draw needn't show every extreme that they name: `p_cols`: the 2 coarse tiles in one row differ; among the fine blocks held by the devices of one index of col, every coarse tile is named at least once and at most 16 times, and some tile exactly 16 times. `q_cols`: the 6 coarse tiles in one row differ; every coarse tile appears somewhere.
All inputs are finite; a program needn't handle non-finite values.
Results may differ from a plain program's by a relative error of at most 0.0003.
Values may be sent and summed in bfloat16 or wider, within the bound.
A program may use at most 128 MiB of HBM per device.

v0:
```python
import math

import jax
import jax.numpy as jnp
from jax import lax
from jax.sharding import PartitionSpec as P


def spread_tiles(tile_set, columns, tile_count):
    blocks, per_block, extent, _ = tile_set.shape
    flipped = jnp.swapaxes(tile_set, 2, 3)
    fine_ids = jnp.broadcast_to(jnp.arange(blocks, dtype=jnp.int32)[:, None], (blocks, per_block))
    placed = jnp.zeros((tile_count, extent, blocks, extent), tile_set.dtype)
    placed = placed.at[columns, :, fine_ids, :].set(flipped)
    return placed.reshape(tile_count * extent, blocks * extent)


def fold_tiles(summed, transposed, tile_set, columns):
    blocks, per_block, extent, _ = tile_set.shape
    height = transposed.shape[0]
    bundle = math.gcd(blocks, 8)
    tile_groups = tile_set.reshape(blocks // bundle, bundle, per_block, extent, extent)
    column_groups = columns.reshape(blocks // bundle, bundle * per_block)

    def one_group(running, inputs):
        position, bundle_tiles, coarse_ids = inputs
        offset = position * bundle * extent
        stripe = lax.dynamic_slice_in_dim(transposed, offset, bundle * extent, 1).reshape(
            height, bundle, extent
        )
        product = jnp.einsum(
            "rfa,fkab->rfkb", stripe, bundle_tiles, preferred_element_type=jnp.float32
        )
        tiled = running.reshape(height, -1, extent)
        tiled = tiled.at[:, coarse_ids, :].add(product.reshape(height, bundle * per_block, extent))
        return (tiled.reshape(height, -1), None)

    counter = jnp.arange(blocks // bundle, dtype=jnp.int32)
    summed, _ = lax.scan(one_group, summed, (counter, tile_groups, column_groups))
    return summed


def body(p_tiles, p_cols, q_tiles, q_cols):
    extent = p_tiles.shape[2]
    tile_count = lax.axis_size("row")
    expanded = spread_tiles(p_tiles, p_cols, tile_count)
    transposed = lax.all_to_all(expanded, "row", split_axis=0, concat_axis=1, tiled=True)
    empty = jnp.zeros((transposed.shape[0], tile_count * extent), jnp.float32)
    partial_sum = fold_tiles(
        empty,
        transposed,
        lax.all_gather(q_tiles, "row", axis=0, tiled=True),
        lax.all_gather(q_cols, "row", axis=0, tiled=True),
    )
    return lax.psum_scatter(partial_sum, "col", scatter_dimension=1, tiled=True)


def solution(mesh):
    placed = (
        P(("row", "col"), None, None, None),
        P(("row", "col"), None),
        P(("row", "col"), None, None, None),
        P(("row", "col"), None),
    )
    return jax.shard_map(
        body, mesh=mesh, in_specs=placed, out_specs=P("row", "col"), check_vma=False
    )
```

profile of v0, /device:TPU:32, one launch (start us, length us, event | category | flops | bytes accessed | tf_op | source)
XLA Modules:
  0.0 603.4 jit_solution(11690526982969184347)
XLA Ops:
  9.3 3.0 broadcast_in_dim.18
  14.5 6.5 %copy.24 = bf16[32,128,4,128]{1,3,2,0:T(8,128)(2,1)} copy(bf16[32,128,4,128]{3,1,2,0:T(8,128)(2,1)} %scatter_fusion.1) | data formatting | bytes 8388608 | tf_op jit(solution)/shard_map/scatter | solution.py:14
  21.0 11.4 %all-to-all-start = ((bf16[32,128,512]{1,2,0:T(8,128)(2,1)}), bf16[32,128,512]{1,2,0:T(8,128)(2,1)}, u32[]{:S(2)}, u32[]{:S(2)}) async-start(bf16[32,128,512]{1,2,0:T(8,128)(2,1)} %bitcast.65), calls=%async_computation | async-start | bytes 8388608 | tf_op jit(solution)/shard_map/all_to_all | solution.py:47
  32.4 152.1 %all-gather = s32[32,4,6]{2,1,0:T(4,128)S(1)} all-gather(s32[1,4,6]{2,1,0:T(4,128)S(1)} %bitcast.68), channel_id=1, replica_groups=mesh['row'=32,'col'=8] {'row'}, dimensions={0}, use_global_device_ids=true | all-gather | bytes 3168 | tf_op jit(solution)/shard_map/all_gather | solution.py:53
  184.7 77.9 %all-gather.3.cloned.1.call-done = bf16[128,6,128,128]{3,2,1,0:T(8,128)(2,1)} async-done(((bf16[4,6,128,128]{3,2,1,0:T(8,128)(2,1)}), bf16[128,6,128,128]{3,2,1,0:T(8,128)(2,1)}) %all-gather.3.cloned.1.call-update) | async-done | bytes 25165840 | tf_op jit(solution)/shard_map/all_gather | solution.py:52
  264.0 274.9 %while.12 = (s32[]{:T(128)}, f32[128,4096]{0,1:T(8,128)}, s32[16,48]{1,0:T(8,128)S(1)}, bf16[16,8,6,128,128]{4,3,2,1,0:T(8,128)(2,1)}, s32[16]{0:T(128)S(1)}, /*...) while((s32[]{:T(128)}, f32[128,4096]{0,1:T(8,128)}, ...), condition=%wide.region_3.4_spmd, body=%wide.region_1.3_spmd.sunk | while | flops 202113168 | bytes 29623528 | solution.py:39
  272.6 6.7 %scatter_fusion = f32[128,32,128]{2,0,1:T(8,128)S(1)} fusion(f32[128,32,128]{2,0,1:T(8,128)S(1)} %copy.34, s32[48]{0:T(128)S(1)} %fusion.16, f32[48,128,128]{2,1,0:T(8,128)} %bitcast.61), kind=kCustom, calls=%fused_computation.clone.1 | custom fusion | flops 786432 | bytes 9437376 | tf_op jit(solution)/shard_map/while/body/eval_jaxpr/scatter-add | solution.py:35
  289.8 6.7 %scatter_fusion = f32[128,32,128]{2,0,1:T(8,128)S(1)} fusion(f32[128,32,128]{2,0,1:T(8,128)S(1)} %copy.34, s32[48]{0:T(128)S(1)} %fusion.16, f32[48,128,128]{2,1,0:T(8,128)} %bitcast.61), kind=kCustom, calls=%fused_computation.clone.1 | custom fusion | flops 786432 | bytes 9437376 | tf_op jit(solution)/shard_map/while/body/eval_jaxpr/scatter-add | solution.py:35
  307.0 6.7 %scatter_fusion = f32[128,32,128]{2,0,1:T(8,128)S(1)} fusion(f32[128,32,128]{2,0,1:T(8,128)S(1)} %copy.34, s32[48]{0:T(128)S(1)} %fusion.16, f32[48,128,128]{2,1,0:T(8,128)} %bitcast.61), kind=kCustom, calls=%fused_computation.clone.1 | custom fusion | flops 786432 | bytes 9437376 | tf_op jit(solution)/shard_map/while/body/eval_jaxpr/scatter-add | solution.py:35
  324.2 6.7 %scatter_fusion = f32[128,32,128]{2,0,1:T(8,128)S(1)} fusion(f32[128,32,128]{2,0,1:T(8,128)S(1)} %copy.34, s32[48]{0:T(128)S(1)} %fusion.16, f32[48,128,128]{2,1,0:T(8,128)} %bitcast.61), kind=kCustom, calls=%fused_computation.clone.1 | custom fusion | flops 786432 | bytes 9437376 | tf_op jit(solution)/shard_map/while/body/eval_jaxpr/scatter-add | solution.py:35
  341.3 6.7 %scatter_fusion = f32[128,32,128]{2,0,1:T(8,128)S(1)} fusion(f32[128,32,128]{2,0,1:T(8,128)S(1)} %copy.34, s32[48]{0:T(128)S(1)} %fusion.16, f32[48,128,128]{2,1,0:T(8,128)} %bitcast.61), kind=kCustom, calls=%fused_computation.clone.1 | custom fusion | flops 786432 | bytes 9437376 | tf_op jit(solution)/shard_map/while/body/eval_jaxpr/scatter-add | solution.py:35
  358.5 6.7 %scatter_fusion = f32[128,32,128]{2,0,1:T(8,128)S(1)} fusion(f32[128,32,128]{2,0,1:T(8,128)S(1)} %copy.34, s32[48]{0:T(128)S(1)} %fusion.16, f32[48,128,128]{2,1,0:T(8,128)} %bitcast.61), kind=kCustom, calls=%fused_computation.clone.1 | custom fusion | flops 786432 | bytes 9437376 | tf_op jit(solution)/shard_map/while/body/eval_jaxpr/scatter-add | solution.py:35
  375.7 6.7 %scatter_fusion = f32[128,32,128]{2,0,1:T(8,128)S(1)} fusion(f32[128,32,128]{2,0,1:T(8,128)S(1)} %copy.34, s32[48]{0:T(128)S(1)} %fusion.16, f32[48,128,128]{2,1,0:T(8,128)} %bitcast.61), kind=kCustom, calls=%fused_computation.clone.1 | custom fusion | flops 786432 | bytes 9437376 | tf_op jit(solution)/shard_map/while/body/eval_jaxpr/scatter-add | solution.py:35
  392.9 6.7 %scatter_fusion = f32[128,32,128]{2,0,1:T(8,128)S(1)} fusion(f32[128,32,128]{2,0,1:T(8,128)S(1)} %copy.34, s32[48]{0:T(128)S(1)} %fusion.16, f32[48,128,128]{2,1,0:T(8,128)} %bitcast.61), kind=kCustom, calls=%fused_computation.clone.1 | custom fusion | flops 786432 | bytes 9437376 | tf_op jit(solution)/shard_map/while/body/eval_jaxpr/scatter-add | solution.py:35
  410.1 6.7 %scatter_fusion = f32[128,32,128]{2,0,1:T(8,128)S(1)} fusion(f32[128,32,128]{2,0,1:T(8,128)S(1)} %copy.34, s32[48]{0:T(128)S(1)} %fusion.16, f32[48,128,128]{2,1,0:T(8,128)} %bitcast.61), kind=kCustom, calls=%fused_computation.clone.1 | custom fusion | flops 786432 | bytes 9437376 | tf_op jit(solution)/shard_map/while/body/eval_jaxpr/scatter-add | solution.py:35
  427.3 6.7 %scatter_fusion = f32[128,32,128]{2,0,1:T(8,128)S(1)} fusion(f32[128,32,128]{2,0,1:T(8,128)S(1)} %copy.34, s32[48]{0:T(128)S(1)} %fusion.16, f32[48,128,128]{2,1,0:T(8,128)} %bitcast.61), kind=kCustom, calls=%fused_computation.clone.1 | custom fusion | flops 786432 | bytes 9437376 | tf_op jit(solution)/shard_map/while/body/eval_jaxpr/scatter-add | solution.py:35
  444.4 6.7 %scatter_fusion = f32[128,32,128]{2,0,1:T(8,128)S(1)} fusion(f32[128,32,128]{2,0,1:T(8,128)S(1)} %copy.34, s32[48]{0:T(128)S(1)} %fusion.16, f32[48,128,128]{2,1,0:T(8,128)} %bitcast.61), kind=kCustom, calls=%fused_computation.clone.1 | custom fusion | flops 786432 | bytes 9437376 | tf_op jit(solution)/shard_map/while/body/eval_jaxpr/scatter-add | solution.py:35
  461.6 6.7 %scatter_fusion = f32[128,32,128]{2,0,1:T(8,128)S(1)} fusion(f32[128,32,128]{2,0,1:T(8,128)S(1)} %copy.34, s32[48]{0:T(128)S(1)} %fusion.16, f32[48,128,128]{2,1,0:T(8,128)} %bitcast.61), kind=kCustom, calls=%fused_computation.clone.1 | custom fusion | flops 786432 | bytes 9437376 | tf_op jit(solution)/shard_map/while/body/eval_jaxpr/scatter-add | solution.py:35
  478.8 6.7 %scatter_fusion = f32[128,32,128]{2,0,1:T(8,128)S(1)} fusion(f32[128,32,128]{2,0,1:T(8,128)S(1)} %copy.34, s32[48]{0:T(128)S(1)} %fusion.16, f32[48,128,128]{2,1,0:T(8,128)} %bitcast.61), kind=kCustom, calls=%fused_computation.clone.1 | custom fusion | flops 786432 | bytes 9437376 | tf_op jit(solution)/shard_map/while/body/eval_jaxpr/scatter-add | solution.py:35
  496.0 6.7 %scatter_fusion = f32[128,32,128]{2,0,1:T(8,128)S(1)} fusion(f32[128,32,128]{2,0,1:T(8,128)S(1)} %copy.34, s32[48]{0:T(128)S(1)} %fusion.16, f32[48,128,128]{2,1,0:T(8,128)} %bitcast.61), kind=kCustom, calls=%fused_computation.clone.1 | custom fusion | flops 786432 | bytes 9437376 | tf_op jit(solution)/shard_map/while/body/eval_jaxpr/scatter-add | solution.py:35
  513.2 6.7 %scatter_fusion = f32[128,32,128]{2,0,1:T(8,128)S(1)} fusion(f32[128,32,128]{2,0,1:T(8,128)S(1)} %copy.34, s32[48]{0:T(128)S(1)} %fusion.16, f32[48,128,128]{2,1,0:T(8,128)} %bitcast.61), kind=kCustom, calls=%fused_computation.clone.1 | custom fusion | flops 786432 | bytes 9437376 | tf_op jit(solution)/shard_map/while/body/eval_jaxpr/scatter-add | solution.py:35
  530.3 6.7 %scatter_fusion = f32[128,32,128]{2,0,1:T(8,128)S(1)} fusion(f32[128,32,128]{2,0,1:T(8,128)S(1)} %copy.34, s32[48]{0:T(128)S(1)} %fusion.16, f32[48,128,128]{2,1,0:T(8,128)} %bitcast.61), kind=kCustom, calls=%fused_computation.clone.1 | custom fusion | flops 786432 | bytes 9437376 | tf_op jit(solution)/shard_map/while/body/eval_jaxpr/scatter-add | solution.py:35
  538.9 2.9 copy.26
  541.9 54.7 %reduce-scatter.2.cloned.1.call-done = f32[128,512]{1,0:T(8,128)} async-done(((f32[128,4096]{1,0:T(8,128)}), f32[128,512]{1,0:T(8,128)}) %reduce-scatter.2.cloned.1.call-update) | async-done | bytes 262160 | tf_op jit(solution)/shard_map/reduce_scatter | solution.py:55
  (127 shorter events, 163.2 us)
Async XLA Ops:
  6.5 256.0 %all-gather.3.cloned.1.call-start = ((), (), s32[]{:S(2)}) async-start(), calls=%async_computation.2 | async-start | bytes 25952256 | tf_op jit(solution)/shard_map/all_gather | solution.py:52
  21.0 11.4 %copy-start = (s32[4,6]{1,0:T(4,128)S(1)}, s32[4,6]{1,0:T(4,128)}, u32[]{:S(2)}) copy-start(s32[4,6]{1,0:T(4,128)} %param.9) | copy-start | bytes 292
  21.0 163.7 %all-to-all-start = ((bf16[32,128,512]{1,2,0:T(8,128)(2,1)}), bf16[32,128,512]{1,2,0:T(8,128)(2,1)}, u32[]{:S(2)}, u32[]{:S(2)}) async-start(bf16[32,128,512]{1,2,0:T(8,128)(2,1)} %bitcast.65), calls=%async_computation | async-start | bytes 8388608 | tf_op jit(solution)/shard_map/all_to_all | solution.py:47
  32.4 564.2 %reduce-scatter.2.cloned.1.call-start = ((), (), s32[]{:S(2)}) async-start(), calls=%async_computation.3 | async-start | bytes 2359296 | tf_op jit(solution)/shard_map/reduce_scatter | solution.py:55
Sparse Core Ops, SparseCore 0:
  10.1 252.3 all-gather.2
  542.0 54.5 reduce-scatter.1
where the time goes:
time: 608 us; the launch traced here: 603 us
  blocking collectives  152 us (25%)
  local copies, waits for them, and re-layouts  141 us (23%)
  waiting for transfers between devices  133 us (22%)
  other arithmetic  109 us (18%)
  matrix products  33 us (5%)
  between operations  13.4 us (2%)
  starting transfers between devices  11.4 us (2%)
  loops' own time  10.5 us (2%)
    all_gather x1, blocking collectives, body(): lax.all_gather(q_cols, 'row', axis=0, tiled=True)  152 us
    scatter-add x16, other arithmetic, one_group(): tiled.at[:, coarse_ids, :]  108 us
    all_gather x1, waiting for transfers between devices, body(): lax.all_gather(q_tiles, 'row', axis=0, tiled=True)  77.9 us
    reduce_scatter x1, waiting for transfers between devices, body(): return lax.psum_scatter(partial_sum, 'col', scatter_dimension=1, tiled=True)  54.7 us
    reshape x16, local copies, waits for them, and re-layouts, one_group(): product.reshape(height, bundle * per_block, extent)  37.8 us
    dot_general x16, matrix products, one_group(): jnp.einsum('rfa,fkab->rfkb', stripe, bundle_tiles, preferred_element_type...  33 us
    reshape x16, local copies, waits for them, and re-layouts, one_group(): tiled = running.reshape(height, -1, extent)  30.7 us
    scatter-add x16, local copies, waits for them, and re-layouts, one_group(): tiled.at[:, coarse_ids, :]  29.2 us
  transfers between devices with their start and end apart: 3, of which 2 were waited for; matrix products, arithmetic and copies ran while one was open for 2% of the time, Pallas kernels for 0%

commit v1 on v0

v1 whole, which is shorter than its diff:
```python
import functools

import jax
import jax.numpy as jnp
from jax import lax
from jax.experimental import pallas as pl
from jax.experimental.pallas import tpu as pltpu
from jax.sharding import PartitionSpec as P

MESH = pl.DeviceIdType.MESH
BF16, F32 = jnp.bfloat16, jnp.float32
ANY = pl.BlockSpec(memory_space=pl.ANY)
VMEM = pl.BlockSpec(memory_space=pltpu.VMEM)
SMEM = pl.BlockSpec(memory_space=pltpu.SMEM)
RECORD = 640


def place():
    row, col = lax.axis_index("row"), lax.axis_index("col")
    core, z = lax.rem(row, 2), lax.rem(lax.div(row, 2), 8)
    x = lax.div(row, 16) * 2 + lax.rem(col, 2)
    return x, lax.div(col, 2), z, core


def device(x, y, z, core):
    return (lax.div(x, 2) * 16 + z * 2 + core, y * 2 + lax.rem(x, 2))


def shift(v, by, n):
    return lax.rem(v + (by + n), n)


def remote(src, dst, send, recv, where):
    return pltpu.make_async_remote_copy(
        src_ref=src, dst_ref=dst, send_sem=send, recv_sem=recv, device_id=where, device_id_type=MESH
    )


def greet(partners):
    barrier = pltpu.get_barrier_semaphore()
    for partner in partners:
        pl.semaphore_signal(barrier, inc=1, device_id=partner, device_id_type=MESH)
    pl.semaphore_wait(barrier, len(partners))


def gather_kernel(p_ref, q_ref, id_ref, gy, gx, iy, ix, stage, send, recv, local, id_send, id_recv):
    x, y, z, core = place()
    other = 1 - core
    rings = (y, x)

    def member(c, pos, who):
        return device(x, pos, z, who) if c == 0 else device(pos, y, z, who)

    others = [(by, flip) for by in range(4) for flip in range(2) if by or flip]
    partners = [member(0, shift(y, by, 4), other if flip else core) for by, flip in others]
    partners += [member(1, shift(x, by, 4), other if flip else core) for by, flip in others if by]
    greet(partners)

    started = []

    def launch(copy):
        copy.start()
        started.append(copy)

    kept = []

    def stage_block(f):
        for c in range(2):
            for k in range(2):
                stage[c, f, k * 128 : (k + 1) * 128, :] = p_ref[f, k]
        for l in range(6):
            flipped = q_ref[f, l].T
            for c in range(2):
                stage[c, f, 256 + l * 64 : 320 + l * 64, :] = flipped[c * 64 : c * 64 + 64]

    def slot(c, pos, who, h):
        return (gy, gx)[c].at[pos, who, pl.ds(h * 2, 2)]

    def own(c, i, h, pos, who):
        launch(
            remote(
                stage.at[c, pl.ds(h * 2, 2)],
                slot(c, rings[c], core, h),
                send.at[c, i],
                recv.at[c, i],
                member(c, pos, who),
            )
        )

    def forward(c, i, h, src, pos, who):
        launch(
            remote(slot(c, src, core, h), slot(c, src, core, h), send.at[c, i], recv.at[c, i], member(c, pos, who))
        )

    def arrived(c, i, h, src, who):
        ref = slot(c, src, who, h)
        remote(ref, ref, send.at[c, i], recv.at[c, i], member(c, rings[c], other)).wait_recv()

    left = [shift(v, -1, 4) for v in rings]
    right = [shift(v, 1, 4) for v in rings]
    far = [shift(v, 2, 4) for v in rings]
    for f in range(2):
        stage_block(f)
    for c in range(2):
        own(c, 0, 0, right[c], core)
        own(c, 6, 0, rings[c], other)
    for f in range(2, 4):
        stage_block(f)
    for c in range(2):
        own(c, 3, 1, left[c], core)
        own(c, 1, 1, right[c], core)
        own(c, 2, 0, left[c], core)
        own(c, 7, 1, rings[c], other)
    for c in range(2):
        copy = pltpu.make_async_copy(stage.at[c], (gy, gx)[c].at[rings[c], core], local.at[c])
        copy.start()
        kept.append(copy)
        ids = (iy, ix)[c]
        copy = pltpu.make_async_copy(id_ref, ids.at[rings[c], core], local.at[2 + c])
        copy.start()
        kept.append(copy)
        for n, (by, flip) in enumerate(others):
            launch(
                remote(
                    id_ref,
                    ids.at[rings[c], core],
                    id_send.at[c, n],
                    id_recv.at[c, n],
                    member(c, shift(rings[c], by, 4), other if flip else core),
                )
            )
    for c in range(2):
        arrived(c, 0, 0, left[c], core)
        forward(c, 4, 0, left[c], right[c], core)
        forward(c, 8, 0, left[c], rings[c], other)
        arrived(c, 3, 1, right[c], core)
        forward(c, 5, 1, right[c], left[c], core)
        forward(c, 11, 1, right[c], rings[c], other)
    for c in range(2):
        arrived(c, 1, 1, left[c], core)
        forward(c, 9, 1, left[c], rings[c], other)
        arrived(c, 2, 0, right[c], core)
        forward(c, 10, 0, right[c], rings[c], other)
    for c in range(2):
        arrived(c, 4, 0, far[c], core)
        forward(c, 12, 0, far[c], rings[c], other)
        arrived(c, 5, 1, far[c], core)
        forward(c, 13, 1, far[c], rings[c], other)
    for c in range(2):
        for i, h, src in (
            (6, 0, rings[c]),
            (7, 1, rings[c]),
            (8, 0, left[c]),
            (9, 1, left[c]),
            (10, 0, right[c]),
            (11, 1, right[c]),
            (12, 0, far[c]),
            (13, 1, far[c]),
        ):
            arrived(c, i, h, src, other)
        for n, (by, flip) in enumerate(others):
            ref = (iy, ix)[c].at[shift(rings[c], -by, 4), other if flip else core]
            remote(ref, ref, id_send.at[c, n], id_recv.at[c, n], member(c, rings[c], other)).wait_recv()
    for copy in started:
        copy.wait_send()
    for copy in kept:
        copy.wait()


def gather(p_tiles, q_tiles, ids):
    records = jax.ShapeDtypeStruct((4, 2, 4, RECORD, 128), BF16)
    numbers = jax.ShapeDtypeStruct((4, 2, 8, 128), jnp.int32)
    return pl.pallas_call(
        gather_kernel,
        name="gather",
        out_shape=(records, records, numbers, numbers),
        in_specs=[VMEM, VMEM, ANY],
        out_specs=(ANY,) * 4,
        scratch_shapes=[
            pltpu.VMEM((2, 4, RECORD, 128), BF16),
            pltpu.SemaphoreType.DMA((2, 14)),
            pltpu.SemaphoreType.DMA((2, 14)),
            pltpu.SemaphoreType.DMA((4,)),
            pltpu.SemaphoreType.DMA((2, 7)),
            pltpu.SemaphoreType.DMA((2, 7)),
        ],
        compiler_params=pltpu.CompilerParams(
            collective_id=0, has_side_effects=True, vmem_limit_bytes=32 << 20
        ),
    )(p_tiles, q_tiles, ids)


def fold_kernel(iy, ix, gy, gx, out, held, total, sem_in, sem_out):
    x, y, _, core = place()
    x_high, x_low = lax.div(x, 2), lax.rem(x, 2)
    loads = [
        [pltpu.make_async_copy(g.at[s // 2, s % 2], held.at[c, s], sem_in.at[c, s]) for s in range(8)]
        for c, g in enumerate((gy, gx))
    ]
    for c in range(2):
        for s in range(8):
            loads[c][s].start()

    @pl.loop(0, 129)
    def _(n):
        for c in range(2):
            total[c, n] = jnp.zeros((64, 128), F32)

    stores = []
    for c, (ids, g) in enumerate(((iy, gy), (ix, gx))):

        @pl.loop(0, 8)
        def _(s, c=c, ids=ids, g=g):
            ring, who = lax.div(s, 2), lax.rem(s, 2)
            pltpu.make_async_copy(g.at[ring, who], held.at[c, s], sem_in.at[c, s]).wait()

            @pl.loop(0, 4)
            def _(f):
                spots = []
                for l in range(6):
                    tile = ids[ring, who, f, 2 + l]
                    j = lax.rem(tile, 4)
                    tile_y, tile_x = lax.div(tile, 8), lax.rem(lax.div(tile, 4), 2)
                    mine, stop = (tile_y == y, tile_x) if c == 0 else (tile_x == x_low, tile_y)
                    spots.append((mine, j * 32 + stop * 8))
                for k in range(2):
                    tile = ids[ring, who, f, k]
                    tile_x = lax.div(tile, 16)
                    tile_z = lax.rem(lax.div(tile, 2), 8)
                    here = lax.rem(tile, 2) == core
                    if c == 1:
                        here = jnp.logical_and(here, tile_x == x_high)
                    base = tile_z + (tile_x * 16 if c == 0 else 0)

                    @pl.when(here)
                    def _(k=k, base=base):
                        product = jnp.dot(
                            held[c, s, f, 256:RECORD, :],
                            held[c, s, f, k * 128 : (k + 1) * 128, :],
                            preferred_element_type=F32,
                        )
                        for l, (mine, spot) in enumerate(spots):
                            n = jnp.where(mine, spot + base, 128)
                            total[c, n] += product[l * 64 : (l + 1) * 64]

        store = pltpu.make_async_copy(total.at[c, pl.ds(0, 128)], out.at[c], sem_out.at[c])
        store.start()
        stores.append(store)
    for store in stores:
        store.wait()


def fold(iy, ix, gy, gx):
    return pl.pallas_call(
        fold_kernel,
        name="fold",
        out_shape=jax.ShapeDtypeStruct((2, 128, 64, 128), F32),
        in_specs=[SMEM, SMEM, ANY, ANY],
        out_specs=ANY,
        scratch_shapes=[
            pltpu.VMEM((2, 8, 4, RECORD, 128), BF16),
            pltpu.VMEM((2, 129, 64, 128), F32),
            pltpu.SemaphoreType.DMA((2, 8)),
            pltpu.SemaphoreType.DMA((2,)),
        ],
        compiler_params=pltpu.CompilerParams(vmem_limit_bytes=48 << 20),
    )(iy, ix, gy, gx)


def reduce_kernel(part_hbm, out, part, near, full, zbuf, load, s_send, s_recv, z_send, z_recv):
    x, y, z, core = place()
    rings = (x, y)

    def member(c, pos):
        return device(pos, y, z, core) if c == 0 else device(x, pos, z, core)

    ends = [[member(c, shift(rings[c], d, 4)) for d in (1, -1)] for c in range(2)]
    z_ends = [device(x, y, shift(z, d, 8), core) for d in (1, -1)]
    loads = {}
    for j in range(4):
        for c in range(2):
            loads[c, j] = pltpu.make_async_copy(part_hbm.at[c, j], part.at[c, j], load.at[c, j])
            loads[c, j].start()
    greet(ends[0] + ends[1] + z_ends)

    started = []
    pending = {}

    def launch(key, copy):
        copy.start()
        started.append(copy)
        pending[key] = copy

    signs = (1, -1)

    def first(c, d, j):
        at = pl.ds(4 * d, 4)
        return remote(
            part.at[c, j, shift(rings[c], 2, 4), at],
            near.at[c, d, j],
            s_send.at[c, d, j, 0],
            s_recv.at[c, d, j, 0],
            ends[c][d],
        )

    def second(c, d, j, half):
        at = pl.ds(4 * half, 4)
        n = 2 if half == d else 1
        return remote(
            part.at[c, j, shift(rings[c], signs[d], 4), at],
            full.at[c, d, j, at],
            s_send.at[c, d, j, n],
            s_recv.at[c, d, j, n],
            ends[c][d],
        )

    def along_z(c, d, j, step):
        target = shift(z, signs[d] * (5 - step), 8)
        rows = pl.ds(32 * d, 32) if step == 1 else pl.ds(0, 64)
        return remote(
            part.at[c, j, rings[c], target, rows],
            zbuf.at[c, d, j, step - 1, rows],
            z_send.at[c, d, j, step - 1],
            z_recv.at[c, d, j, step - 1],
            z_ends[d],
        )

    both = [(c, d) for c in range(2) for d in range(2)]

    def open_chunk(j):
        for c in range(2):
            loads[c, j].wait()
        for c, d in both:
            launch(("first", c, d, j), first(c, d, j))
        for c, d in both:
            launch(("direct", c, d, j), second(c, d, j, 1 - d))

    def relay_chunk(j):
        for c, d in both:
            pending["first", c, d, j].wait_recv()
            spot = shift(rings[c], signs[d], 4)
            part[c, j, spot, 4 * d : 4 * d + 4] += near[c, d, j]
            launch(("relay", c, d, j), second(c, d, j, d))

    def close_chunk(j):
        for c, d in both:
            pending["direct", c, d, j].wait_recv()
            pending["relay", c, d, j].wait_recv()
        for c in range(2):
            part[c, j, rings[c]] += full[c, 0, j] + full[c, 1, j]

    def z_step(j, step):
        for c, d in both:
            if step > 1:
                pending["z", c, d, j, step - 1].wait_recv()
                target = shift(z, signs[d] * (5 - step), 8)
                rows = pl.ds(32 * d, 32) if step == 2 else pl.ds(0, 64)
                part[c, j, rings[c], target, rows] += zbuf[c, d, j, step - 2, rows]
            if step < 5:
                launch(("z", c, d, j, step), along_z(c, d, j, step))

    def finish_chunk(j):
        tiles = []
        for c in range(2):
            for d in range(2):
                pending["z", c, d, j, 4].wait_recv()
            tiles.append(part[c, j, rings[c], z] + zbuf[c, 0, j, 3] + zbuf[c, 1, j, 3])
        out[:, j * 128 : (j + 1) * 128] = jnp.concatenate(tiles, axis=0).T

    for tick in range(5):
        if tick < 4:
            open_chunk(tick)
        if tick > 0:
            z_step(tick - 1, 1)
            z_step(tick - 1, 2)
        if tick < 4:
            relay_chunk(tick)
        if tick > 0:
            z_step(tick - 1, 3)
            z_step(tick - 1, 4)
            finish_chunk(tick - 1)
        if tick < 4:
            close_chunk(tick)
    for copy in started:
        copy.wait_send()


def reduce(partial):
    return pl.pallas_call(
        reduce_kernel,
        name="reduce",
        out_shape=jax.ShapeDtypeStruct((128, 512), F32),
        in_specs=[ANY],
        out_specs=VMEM,
        scratch_shapes=[
            pltpu.VMEM((2, 4, 4, 8, 64, 128), F32),
            pltpu.VMEM((2, 2, 4, 4, 64, 128), F32),
            pltpu.VMEM((2, 2, 4, 8, 64, 128), F32),
            pltpu.VMEM((2, 2, 4, 4, 64, 128), F32),
            pltpu.SemaphoreType.DMA((2, 4)),
            pltpu.SemaphoreType.DMA((2, 2, 4, 3)),
            pltpu.SemaphoreType.DMA((2, 2, 4, 3)),
            pltpu.SemaphoreType.DMA((2, 2, 4, 4)),
            pltpu.SemaphoreType.DMA((2, 2, 4, 4)),
        ],
        compiler_params=pltpu.CompilerParams(
            collective_id=1, has_side_effects=True, vmem_limit_bytes=48 << 20
        ),
    )(partial.reshape(2, 4, 4, 8, 64, 128))


def body(p_tiles, p_cols, q_tiles, q_cols):
    ids = jnp.pad(jnp.concatenate([p_cols, q_cols], axis=1), ((0, 4), (0, 120)))
    gy, gx, iy, ix = gather(p_tiles, q_tiles, ids)
    return reduce(fold(iy, ix, gy, gx))


def solution(mesh):
    placed = (
        P(("row", "col"), None, None, None),
        P(("row", "col"), None),
        P(("row", "col"), None, None, None),
        P(("row", "col"), None),
    )
    return jax.shard_map(
        body, mesh=mesh, in_specs=placed, out_specs=P("row", "col"), check_vma=False
    )
```

time: 608 us -> 135 us (0.22)
  blocking collectives: 152 us -> 0 us
  local copies, waits for them, and re-layouts: 141 us -> 5.93 us
  waiting for transfers between devices: 133 us -> 0 us
  Pallas kernels: 0 us -> 128 us
  other arithmetic: 109 us -> 0.75 us
  matrix products: 33 us -> 0 us
  between operations: 13.4 us -> 0.04 us
  starting transfers between devices: 11.4 us -> 0 us
  loops' own time: 10.5 us -> 0 us
    all_gather x1 -> x0, blocking collectives: 152 us -> none  [body(): lax.all_gather(q_cols, 'row', axis=0, tiled=True)]
    pallas_call x0 -> x3, Pallas kernels: none -> 128 us  [the longest x1 79.2 us: reduce(): pl.pallas_call(reduce_kernel, name='reduce', out_shape=jax.ShapeDtypeStru...]
    scatter-add x16 -> x0, other arithmetic: 108 us -> none  [one_group(): tiled.at[:, coarse_ids, :]]
    all_gather x1 -> x0, waiting for transfers between devices: 77.9 us -> none  [body(): lax.all_gather(q_tiles, 'row', axis=0, tiled=True)]
    reshape x33 -> x0, local copies, waits for them, and re-layouts: 68.6 us -> none  [the longest x16 37.8 us: one_group(): product.reshape(height, bundle * per_block, extent)]
    reduce_scatter x1 -> x0, waiting for transfers between devices: 54.7 us -> none  [body(): return lax.psum_scatter(partial_sum, 'col', scatter_dimension=1, tiled=True)]
    dot_general x16 -> x0, matrix products: 33 us -> none  [one_group(): jnp.einsum('rfa,fkab->rfkb', stripe, bundle_tiles, preferred_element_type...]
    scatter-add x16 -> x0, local copies, waits for them, and re-layouts: 29.2 us -> none  [one_group(): tiled.at[:, coarse_ids, :]]
  transfers between devices with their start and end apart: 3 -> 0, of which waited for: 2 -> 0; matrix products, arithmetic and copies ran while one was open for 2% -> 0% of each run, Pallas kernels for 0% -> 0%
where the time goes in v1:
time: 135 us
  Pallas kernels  128 us (95%)
  local copies, waits for them, and re-layouts  5.93 us (4%)
    pallas_call x1, Pallas kernels, reduce(): pl.pallas_call(reduce_kernel, name='reduce', out_shape=jax.ShapeDtypeStru...  79.2 us
    pallas_call x1, Pallas kernels, gather(): pl.pallas_call(gather_kernel, name='gather', out_shape=(records, records,...  32.1 us
    pallas_call x1, Pallas kernels, fold(): pl.pallas_call(fold_kernel, name='fold', out_shape=jax.ShapeDtypeStruct((...  16.6 us
    unnamed x8, local copies, waits for them, and re-layouts  5.93 us

profile of v1, /device:TPU:32, one launch (start us, length us, event | category | flops | bytes accessed | tf_op | source)
XLA Modules:
  0.0 134.6 jit_solution(3083162328528918860)
XLA Ops:
  0.0 0.8 copy.5
  0.8 0.8 pad_add_fusion
  1.5 0.0 copy-start.1
  1.5 1.1 copy-done.1
  2.7 0.0 copy-start.2
  2.7 0.9 copy-done.2
  3.6 32.1 %gather.1 = (bf16[4,2,4,640,128]{4,3,2,1,0:T(8,128)(2,1)S(1)}, bf16[4,2,4,640,128]{4,3,2,1,0:T(8,128)(2,1)S(1)}, s32[4,2,8,128]{3,2,1,0:T(8,128)S(1)}, s32[4,2,8,128]{3,2,1,0:T(8,128)S(1)}) custom-call(bf16[4,2,128,128]{3,2,1,0:T(8,128)(2,1)S(1)} %copy-done.2, bf16[4,6,128,128]{3,2,1,0:T(8,128)(2,1)S(1)} %copy-done.1, s32[8,128]{1,0:T(8,128)S(1)} %pad.4.id_ref), custom_call_target="tpu_custom_call" | custom-call | tf_op jit(solution)/shard_map/gather/pallas_call | solution.py:173
  35.7 0.0 copy-start
  35.7 2.4 %copy-done = bf16[4,2,4,640,128]{4,3,2,1,0:T(8,128)(2,1)} copy-done((bf16[4,2,4,640,128]{4,3,2,1,0:T(8,128)(2,1)}, bf16[4,2,4,640,128]{4,3,2,1,0:T(8,128)(2,1)S(1)}, u32[]{:S(2)}) %copy-start) | copy-done | bytes 5242904
  38.1 16.6 %fold.1 = f32[2,128,64,128]{3,2,1,0:T(8,128)} custom-call(s32[4,2,8,128]{3,2,1,0:T(8,128)S(1)} %get-tuple-element.9.iy, s32[4,2,8,128]{3,2,1,0:T(8,128)S(1)} %get-tuple-element.10.ix, bf16[4,2,4,640,128]{4,3,2,1,0:T(8,128)(2,1)S(1)} %get-tuple-element.11.gy, bf16[4,2,4,640,128]{4,3,2,1,0:T(8,128)(2,1)} %copy-done), custom_call_target="tpu_custom_call" | custom-call | tf_op jit(solution)/shard_map/fold/pallas_call | solution.py:254
  54.6 79.2 %reduce.1 = f32[128,512]{1,0:T(8,128)S(1)} custom-call(f32[2,4,4,8,64,128]{5,4,3,2,1,0:T(8,128)} %bitcast.1), custom_call_target="tpu_custom_call" | custom-call | tf_op jit(solution)/shard_map/reduce/pallas_call | solution.py:389
  133.9 0.7 copy.7
  (1 shorter events, 0.0 us)
Async XLA Ops:
  1.5 1.1 copy-start.1
  2.7 0.9 copy-start.2
  35.7 2.4 %copy-start = (bf16[4,2,4,640,128]{4,3,2,1,0:T(8,128)(2,1)}, bf16[4,2,4,640,128]{4,3,2,1,0:T(8,128)(2,1)S(1)}, u32[]{:S(2)}) copy-start(bf16[4,2,4,640,128]{4,3,2,1,0:T(8,128)(2,1)S(1)} %get-tuple-element.12.gx) | copy-start | bytes 15728644

commit v2 on v0

v2 whole, which is shorter than its diff:
```python
import jax
import jax.numpy as jnp
from jax import lax
from jax.experimental import pallas as pl
from jax.experimental.pallas import tpu as pltpu
from jax.sharding import PartitionSpec as P

MESH = pl.DeviceIdType.MESH
BF16, F32 = jnp.bfloat16, jnp.float32
ANY = pl.BlockSpec(memory_space=pl.ANY)
VMEM = pl.BlockSpec(memory_space=pltpu.VMEM)
RECORD = 640
LOAD = 48
NONE = 8 * LOAD


def place():
    row, col = lax.axis_index("row"), lax.axis_index("col")
    core, z = lax.rem(row, 2), lax.rem(lax.div(row, 2), 8)
    x = lax.div(row, 16) * 2 + lax.rem(col, 2)
    return x, lax.div(col, 2), z, core


def device(x, y, z, core):
    return (lax.div(x, 2) * 16 + z * 2 + core, y * 2 + lax.rem(x, 2))


def shift(v, by, n):
    return lax.rem(v + (by + n), n)


def remote(src, dst, send, recv, where):
    return pltpu.make_async_remote_copy(
        src_ref=src, dst_ref=dst, send_sem=send, recv_sem=recv, device_id=where, device_id_type=MESH
    )


def greet(partners):
    barrier = pltpu.get_barrier_semaphore()
    for partner in partners:
        pl.semaphore_signal(barrier, inc=1, device_id=partner, device_id_type=MESH)
    pl.semaphore_wait(barrier, len(partners))


def kernel(
    p_hbm, q_hbm, id_hbm, out,
    p_in, q_in, held, ids, table, marks, run, part, near, full, zbuf,
    in_sem, g_send, g_recv, id_send, id_recv, s_send, s_recv, z_send, z_recv,
):
    x, y, z, core = place()
    other = 1 - core
    gather_rings, reduce_rings = (y, x), (x, y)

    def along_y(pos, who):
        return device(x, pos, z, who)

    def along_x(pos, who):
        return device(pos, y, z, who)

    gather_member, reduce_member = (along_y, along_x), (along_x, along_y)
    z_ends = [device(x, y, shift(z, d, 8), core) for d in (1, -1)]
    others = [(by, flip) for by in range(4) for flip in range(2) if by or flip]

    inputs = []
    for f in range(4):
        inputs.append(pltpu.make_async_copy(q_hbm.at[f], q_in.at[f], in_sem.at[f]))
    inputs.append(pltpu.make_async_copy(p_hbm, p_in, in_sem.at[4]))
    inputs.append(pltpu.make_async_copy(id_hbm, ids.at[0, 0], in_sem.at[5]))
    inputs.append(pltpu.make_async_copy(id_hbm, ids.at[1, 0], in_sem.at[6]))
    for copy in inputs:
        copy.start()

    partners = [along_y(shift(y, by, 4), other if flip else core) for by, flip in others]
    partners += [along_x(shift(x, by, 4), other if flip else core) for by, flip in others if by]
    greet(partners + z_ends)

    started = []

    def launch(copy):
        copy.start()
        started.append(copy)
        return copy

    slot = {0: 0, 1: 2, 3: 4, 2: 6}
    inputs[5].wait()
    inputs[6].wait()
    for c in range(2):
        for n, (by, flip) in enumerate(others):
            who = gather_member[c](shift(gather_rings[c], by, 4), other if flip else core)
            launch(remote(ids.at[c, 0], ids.at[c, slot[by] + flip], id_send.at[c, n], id_recv.at[c, n], who))

    def stage_block(f):
        inputs[f].wait()
        for c in range(2):
            for k in range(2):
                held[c, 0, f, k * 128 : (k + 1) * 128, :] = p_in[f, k]
        for l in range(6):
            flipped = q_in[f, l].T
            for c in range(2):
                held[c, 0, f, 256 + l * 64 : 320 + l * 64, :] = flipped[c * 64 : c * 64 + 64]

    def send(c, i, h, source, target, by, flip=False):
        at = pl.ds(h * 2, 2)
        who = gather_member[c](shift(gather_rings[c], by, 4), other if flip else core)
        launch(remote(held.at[c, source, at], held.at[c, target, at], g_send.at[c, i], g_recv.at[c, i], who))

    def arrived(c, i, h, target):
        ref = held.at[c, target, pl.ds(h * 2, 2)]
        remote(ref, ref, g_send.at[c, i], g_recv.at[c, i], gather_member[c](gather_rings[c], other)).wait_recv()

    inputs[4].wait()
    for f in range(2):
        stage_block(f)
    for c in range(2):
        send(c, 0, 0, 0, 2, 1)
        send(c, 6, 0, 0, 1, 0, True)
    for f in range(2, 4):
        stage_block(f)
    for c in range(2):
        send(c, 3, 1, 0, 4, -1)
        send(c, 1, 1, 0, 2, 1)
        send(c, 2, 0, 0, 4, -1)
        send(c, 7, 1, 0, 1, 0, True)

    for c in range(2):
        for n, (by, flip) in enumerate(others):
            ref = ids.at[c, slot[by] + flip]
            remote(ref, ref, id_send.at[c, n], id_recv.at[c, n], gather_member[c](gather_rings[c], other)).wait_recv()
    lane = lax.broadcasted_iota(jnp.int32, (8, 128), 1)
    below = lax.broadcasted_iota(jnp.int32, (LOAD, 128), 0)
    beside = lax.broadcasted_iota(jnp.int32, (LOAD, 128), 1)
    for c in range(2):
        rows = jnp.concatenate([ids[c, t, 0:1, :] for t in range(8)], axis=0)
        cols = jnp.concatenate([ids[c, t, 1:2, :] for t in range(8)], axis=0)
        mine = jnp.logical_and((rows & 1) == core, lane < LOAD)
        tile_x, tile_z = rows >> 4, (rows >> 1) & 7
        stop_y, stop_x, j = cols >> 3, (cols >> 2) & 1, cols & 3
        if c == 0:
            mine = jnp.logical_and(mine, stop_y == y)
            target = j * 32 + (tile_x * 2 + stop_x) * 8 + tile_z
        else:
            mine = jnp.logical_and(mine, jnp.logical_and(tile_x == lax.div(x, 2), stop_x == lax.rem(x, 2)))
            target = j * 32 + stop_y * 8 + tile_z
        target = jnp.where(mine, target, -1)
        flat = jnp.where(mine, target, -2).T[0:LOAD]
        last = jnp.full((1, 128), -1, jnp.int32)
        for t in range(8):
            same = jnp.broadcast_to(flat[:, t : t + 1], (LOAD, 128)) == beside
            last = jnp.maximum(last, jnp.max(jnp.where(same, below + t * LOAD, -1), axis=0, keepdims=True))
            found = jnp.full((1, 128), -1, jnp.int32)
            mark = jnp.broadcast_to(target[t : t + 1], (LOAD, 128))
            for u in range(t + 1):
                same = jnp.broadcast_to(flat[:, u : u + 1], (LOAD, 128)) == mark
                if u == t:
                    same = jnp.logical_and(same, below < beside)
                found = jnp.maximum(found, jnp.max(jnp.where(same, below + u * LOAD, -1), axis=0, keepdims=True))
            table[c, t : t + 1, :] = jnp.where(found < 0, NONE, found)
        table[c, 8:9, :] = jnp.where(last < 0, NONE, last)
        table[c, 9:16, :] = jnp.zeros((7, 128), jnp.int32)
        run[c, NONE] = jnp.zeros((64, 128), F32)
    copy = pltpu.make_async_copy(table, marks, in_sem.at[7])
    copy.start()
    copy.wait()

    def multiply(c, t):
        @pl.loop(0, 4)
        def _(f):
            pair = jnp.concatenate([held[c, t, f, 0:128, :], held[c, t, f, 128:256, :]], axis=1)
            product = jnp.dot(held[c, t, f, 256:RECORD, :], pair, preferred_element_type=F32)
            for k in range(2):
                sums = []
                for l in range(6):
                    before = run[c, marks[c, t, f * 12 + k * 6 + l]]
                    sums.append(product[l * 64 : (l + 1) * 64, k * 128 : (k + 1) * 128] + before)
                for l in range(6):
                    run[c, t * LOAD + f * 12 + k * 6 + l] = sums[l]

    for c in range(2):
        multiply(c, 0)
    for c in range(2):
        arrived(c, 6, 0, 1)
        arrived(c, 7, 1, 1)
        multiply(c, 1)
    for c in range(2):
        arrived(c, 0, 0, 2)
        send(c, 4, 0, 2, 6, 1)
        send(c, 8, 0, 2, 3, 0, True)
        arrived(c, 3, 1, 4)
        send(c, 5, 1, 4, 6, -1)
        send(c, 11, 1, 4, 5, 0, True)
    for c in range(2):
        arrived(c, 1, 1, 2)
        send(c, 9, 1, 2, 3, 0, True)
        arrived(c, 2, 0, 4)
        send(c, 10, 0, 4, 5, 0, True)
    for c in range(2):
        multiply(c, 2)
    for c in range(2):
        arrived(c, 8, 0, 3)
        arrived(c, 9, 1, 3)
        multiply(c, 3)
    for c in range(2):
        multiply(c, 4)
    for c in range(2):
        arrived(c, 10, 0, 5)
        arrived(c, 11, 1, 5)
        multiply(c, 5)
    for c in range(2):
        arrived(c, 4, 0, 6)
        send(c, 12, 0, 6, 7, 0, True)
        arrived(c, 5, 1, 6)
        send(c, 13, 1, 6, 7, 0, True)
    for c in range(2):
        multiply(c, 6)
    for c in range(2):
        arrived(c, 12, 0, 7)
        arrived(c, 13, 1, 7)
        multiply(c, 7)

    rings, signs = reduce_rings, (1, -1)
    ends = [[reduce_member[c](shift(rings[c], d, 4), core) for d in signs] for c in range(2)]
    pending = {}

    def first(c, d, j):
        at = pl.ds(4 * d, 4)
        return remote(
            part.at[c, j, shift(rings[c], 2, 4), at],
            near.at[c, d, j],
            s_send.at[c, d, j, 0],
            s_recv.at[c, d, j, 0],
            ends[c][d],
        )

    def second(c, d, j, half):
        at = pl.ds(4 * half, 4)
        n = 2 if half == d else 1
        return remote(
            part.at[c, j, shift(rings[c], signs[d], 4), at],
            full.at[c, d, j, at],
            s_send.at[c, d, j, n],
            s_recv.at[c, d, j, n],
            ends[c][d],
        )

    def along_z(c, d, j, step):
        target = shift(z, signs[d] * (5 - step), 8)
        rows = pl.ds(32 * d, 32) if step == 1 else pl.ds(0, 64)
        return remote(
            part.at[c, j, rings[c], target, rows],
            zbuf.at[c, d, j, step - 1, rows],
            z_send.at[c, d, j, step - 1],
            z_recv.at[c, d, j, step - 1],
            z_ends[d],
        )

    both = [(c, d) for c in range(2) for d in range(2)]

    def open_chunk(j):
        for c in range(2):

            @pl.loop(0, 32)
            def _(n, c=c):
                part[c, j, lax.div(n, 8), lax.rem(n, 8)] = run[c, marks[c, 8, j * 32 + n]]

        for c, d in both:
            pending["first", c, d, j] = launch(first(c, d, j))
        for c, d in both:
            pending["direct", c, d, j] = launch(second(c, d, j, 1 - d))

    def relay_chunk(j):
        for c, d in both:
            pending["first", c, d, j].wait_recv()
            spot = shift(rings[c], signs[d], 4)
            part[c, j, spot, 4 * d : 4 * d + 4] += near[c, d, j]
            pending["relay", c, d, j] = launch(second(c, d, j, d))

    def close_chunk(j):
        for c, d in both:
            pending["direct", c, d, j].wait_recv()
            pending["relay", c, d, j].wait_recv()
        for c in range(2):
            part[c, j, rings[c]] += full[c, 0, j] + full[c, 1, j]

    def z_step(j, step):
        for c, d in both:
            if step > 1:
                pending["z", c, d, j, step - 1].wait_recv()
                target = shift(z, signs[d] * (5 - step), 8)
                rows = pl.ds(32 * d, 32) if step == 2 else pl.ds(0, 64)
                part[c, j, rings[c], target, rows] += zbuf[c, d, j, step - 2, rows]
            if step < 5:
                pending["z", c, d, j, step] = launch(along_z(c, d, j, step))

    def finish_chunk(j):
        tiles = []
        for c in range(2):
            for d in range(2):
                pending["z", c, d, j, 4].wait_recv()
            tiles.append(part[c, j, rings[c], z] + zbuf[c, 0, j, 3] + zbuf[c, 1, j, 3])
        out[:, j * 128 : (j + 1) * 128] = jnp.concatenate(tiles, axis=0).T

    for tick in range(5):
        if tick < 4:
            open_chunk(tick)
        if tick > 0:
            z_step(tick - 1, 1)
            z_step(tick - 1, 2)
        if tick < 4:
            relay_chunk(tick)
        if tick > 0:
            z_step(tick - 1, 3)
            z_step(tick - 1, 4)
            finish_chunk(tick - 1)
        if tick < 4:
            close_chunk(tick)
    for copy in started:
        copy.wait_send()


def body(p_tiles, p_cols, q_tiles, q_cols):
    rows = jnp.broadcast_to(p_cols[:, :, None], (4, 2, 6)).reshape(1, LOAD)
    cols = jnp.broadcast_to(q_cols[:, None, :], (4, 2, 6)).reshape(1, LOAD)
    ids = jnp.pad(jnp.concatenate([rows, cols], axis=0), ((0, 6), (0, 128 - LOAD)))
    dma = pltpu.SemaphoreType.DMA
    return pl.pallas_call(
        kernel,
        name="coarse",
        out_shape=jax.ShapeDtypeStruct((128, 512), F32),
        in_specs=[ANY, ANY, ANY],
        out_specs=VMEM,
        scratch_shapes=[
            pltpu.VMEM((4, 2, 128, 128), BF16),
            pltpu.VMEM((4, 6, 128, 128), BF16),
            pltpu.VMEM((2, 8, 4, RECORD, 128), BF16),
            pltpu.VMEM((2, 8, 8, 128), jnp.int32),
            pltpu.VMEM((2, 16, 128), jnp.int32),
            pltpu.SMEM((2, 16, 128), jnp.int32),
            pltpu.VMEM((2, NONE + 1, 64, 128), F32),
            pltpu.VMEM((2, 4, 4, 8, 64, 128), F32),
            pltpu.VMEM((2, 2, 4, 4, 64, 128), F32),
            pltpu.VMEM((2, 2, 4, 8, 64, 128), F32),
            pltpu.VMEM((2, 2, 4, 4, 64, 128), F32),
            dma((8,)),
            dma((2, 14)),
            dma((2, 14)),
            dma((2, 7)),
            dma((2, 7)),
            dma((2, 2, 4, 3)),
            dma((2, 2, 4, 3)),
            dma((2, 2, 4, 4)),
            dma((2, 2, 4, 4)),
        ],
        compiler_params=pltpu.CompilerParams(
            collective_id=0, has_side_effects=True, vmem_limit_bytes=60 << 20
        ),
    )(p_tiles, q_tiles, ids)


def solution(mesh):
    placed = (
        P(("row", "col"), None, None, None),
        P(("row", "col"), None),
        P(("row", "col"), None, None, None),
        P(("row", "col"), None),
    )
    return jax.shard_map(
        body, mesh=mesh, in_specs=placed, out_specs=P("row", "col"), check_vma=False
    )
```

time: 608 us -> 114 us (0.19)
  blocking collectives: 152 us -> 0 us
  local copies, waits for them, and re-layouts: 141 us -> 3.88 us
  waiting for transfers between devices: 133 us -> 0 us
  Pallas kernels: 0 us -> 110 us
  other arithmetic: 109 us -> 0.01 us
  matrix products: 33 us -> 0 us
  between operations: 13.4 us -> 0.01 us
  starting transfers between devices: 11.4 us -> 0 us
  loops' own time: 10.5 us -> 0 us
    all_gather x1 -> x0, blocking collectives: 152 us -> none  [body(): lax.all_gather(q_cols, 'row', axis=0, tiled=True)]
    pallas_call x0 -> x1, Pallas kernels: none -> 110 us  [body(): pl.pallas_call(kernel, name='coarse', out_shape=jax.ShapeDtypeStruct((128...]
    scatter-add x16 -> x0, other arithmetic: 108 us -> none  [one_group(): tiled.at[:, coarse_ids, :]]
    all_gather x1 -> x0, waiting for transfers between devices: 77.9 us -> none  [body(): lax.all_gather(q_tiles, 'row', axis=0, tiled=True)]
    reshape x33 -> x2, local copies, waits for them, and re-layouts: 68.6 us -> 0.17 us  [the longest x1 0.09 us: body(): cols = jnp.broadcast_to(q_cols[:, None, :], (4, 2, 6)).reshape(1, LOAD)]
    reduce_scatter x1 -> x0, waiting for transfers between devices: 54.7 us -> none  [body(): return lax.psum_scatter(partial_sum, 'col', scatter_dimension=1, tiled=True)]
    dot_general x16 -> x0, matrix products: 33 us -> none  [one_group(): jnp.einsum('rfa,fkab->rfkb', stripe, bundle_tiles, preferred_element_type...]
    scatter-add x16 -> x0, local copies, waits for them, and re-layouts: 29.2 us -> none  [one_group(): tiled.at[:, coarse_ids, :]]
  transfers between devices with their start and end apart: 3 -> 0, of which waited for: 2 -> 0; matrix products, arithmetic and copies ran while one was open for 2% -> 0% of each run, Pallas kernels for 0% -> 0%
where the time goes in v2:
time: 114 us
  Pallas kernels  110 us (96%)
  local copies, waits for them, and re-layouts  3.88 us (3%)
    pallas_call x1, Pallas kernels, body(): pl.pallas_call(kernel, name='coarse', out_shape=jax.ShapeDtypeStruct((128...  110 us
    unnamed x4, local copies, waits for them, and re-layouts  3.03 us

profile of v2, /device:TPU:32, one launch (start us, length us, event | category | flops | bytes accessed | tf_op | source)
XLA Modules:
  0.0 113.7 jit_solution(6457457336331993646)
XLA Ops:
  0.0 0.8 copy.5
  0.8 0.1 broadcast_in_dim.4
  0.8 0.0 copy-start
  0.8 0.1 reshape.8
  0.9 0.6 copy-done
  1.5 0.1 reshape.9
  1.6 0.6 pad.4.id_hbm
  2.2 109.8 %coarse.1 = f32[128,512]{1,0:T(8,128)} custom-call(bf16[4,2,128,128]{3,2,1,0:T(8,128)(2,1)} %p_hbm.1, bf16[4,6,128,128]{3,2,1,0:T(8,128)(2,1)} %q_hbm.1, s32[8,128]{1,0:T(8,128)} %pad.4.id_hbm), custom_call_target="tpu_custom_call" | custom-call | tf_op jit(solution)/shard_map/coarse/pallas_call | solution.py:325
  112.1 1.7 %copy.7 = f32[128,512]{1,0:T(8,128)} copy(f32[128,512]{1,0:T(8,128)} %coarse.1) | data formatting | bytes 524288
  (2 shorter events, 0.0 us)
Async XLA Ops:
  0.8 0.7 copy-start

commit v3 on v2

--- a/solution.py
+++ b/solution.py
@@ -12,6 +12,19 @@
 RECORD = 640
 LOAD = 48
 NONE = 8 * LOAD
+CHUNKS = (
+    (0, 0, 64, True),
+    (1, 0, 64, True),
+    (2, 0, 64, True),
+)
+WIDE = ((3, 0, 64),)
+ORDER = (
+    ("load", 0), ("first", 0), ("wload", 0), ("wz", 0, 1), ("load", 1), ("direct", 0), ("load", 2), ("first", 2),
+    ("wz", 0, 2), ("relay", 0), ("first", 1), ("wz", 0, 3), ("relay", 2), ("close", 0), ("z", 0, 1), ("direct", 2),
+    ("direct", 1), ("wz", 0, 4), ("relay", 1), ("close", 2), ("z", 2, 1), ("z", 0, 2), ("z", 2, 2), ("wring", 0),
+    ("z", 0, 3), ("close", 1), ("z", 1, 1), ("z", 2, 3), ("z", 1, 2), ("z", 2, 4), ("wrelay", 0), ("z", 1, 3),
+    ("z", 0, 4), ("z", 1, 4), ("finish", 0), ("wfinish", 0), ("finish", 2), ("finish", 1),
+)
 
 
 def place():
@@ -44,8 +57,8 @@
 
 def kernel(
     p_hbm, q_hbm, id_hbm, out,
-    p_in, q_in, held, ids, table, marks, run, part, near, full, zbuf,
-    in_sem, g_send, g_recv, id_send, id_recv, s_send, s_recv, z_send, z_recv,
+    p_in, q_in, held, ids, table, marks, run, part, near, full, zbuf, zall, done, wbuf, ring,
+    in_sem, g_send, g_recv, id_send, id_recv, s_send, s_recv, z_send, z_recv, d_send, d_recv, w_send, w_recv, r_send, r_recv,
 ):
     x, y, z, core = place()
     other = 1 - core
@@ -59,6 +72,7 @@
 
     gather_member, reduce_member = (along_y, along_x), (along_x, along_y)
     z_ends = [device(x, y, shift(z, d, 8), core) for d in (1, -1)]
+    z_ring = [device(x, y, shift(z, d, 8), core) for d in range(1, 8)]
     others = [(by, flip) for by in range(4) for flip in range(2) if by or flip]
 
     inputs = []
@@ -72,7 +86,7 @@
 
     partners = [along_y(shift(y, by, 4), other if flip else core) for by, flip in others]
     partners += [along_x(shift(x, by, 4), other if flip else core) for by, flip in others if by]
-    greet(partners + z_ends)
+    greet(partners + z_ring)
 
     started = []
 
@@ -221,98 +235,205 @@
     ends = [[reduce_member[c](shift(rings[c], d, 4), core) for d in signs] for c in range(2)]
     pending = {}
 
-    def first(c, d, j):
-        at = pl.ds(4 * d, 4)
+    def rows_of(i):
+        _, start, count, _ = CHUNKS[i]
+        return pl.ds(start, count)
+
+    def first(c, d, i):
+        j, at = CHUNKS[i][0], pl.ds(4 * d, 4)
         return remote(
-            part.at[c, j, shift(rings[c], 2, 4), at],
-            near.at[c, d, j],
-            s_send.at[c, d, j, 0],
-            s_recv.at[c, d, j, 0],
+            part.at[c, j, shift(rings[c], 2, 4), at, rows_of(i)],
+            near.at[c, d, j, :, rows_of(i)],
+            s_send.at[c, d, i, 0],
+            s_recv.at[c, d, i, 0],
             ends[c][d],
         )
 
-    def second(c, d, j, half):
-        at = pl.ds(4 * half, 4)
+    def second(c, d, i, half):
+        j, at = CHUNKS[i][0], pl.ds(4 * half, 4)
         n = 2 if half == d else 1
         return remote(
-            part.at[c, j, shift(rings[c], signs[d], 4), at],
-            full.at[c, d, j, at],
-            s_send.at[c, d, j, n],
-            s_recv.at[c, d, j, n],
+            part.at[c, j, shift(rings[c], signs[d], 4), at, rows_of(i)],
+            full.at[c, d, j, at, rows_of(i)],
+            s_send.at[c, d, i, n],
+            s_recv.at[c, d, i, n],
             ends[c][d],
         )
 
-    def along_z(c, d, j, step):
+    def along_z(c, d, i, step):
+        j = CHUNKS[i][0]
         target = shift(z, signs[d] * (5 - step), 8)
-        rows = pl.ds(32 * d, 32) if step == 1 else pl.ds(0, 64)
+        _, start, count, _ = CHUNKS[i]
+        rows = pl.ds(start + d * count // 2, count // 2) if step == 1 else pl.ds(start, count)
         return remote(
             part.at[c, j, rings[c], target, rows],
             zbuf.at[c, d, j, step - 1, rows],
-            z_send.at[c, d, j, step - 1],
-            z_recv.at[c, d, j, step - 1],
+            z_send.at[c, d, i, step - 1],
+            z_recv.at[c, d, i, step - 1],
             z_ends[d],
         )
 
+    def straight(c, i, by):
+        j = CHUNKS[i][0]
+        target = shift(z, by, 8)
+        return remote(
+            part.at[c, j, rings[c], target, rows_of(i)],
+            zall.at[c, by - 1, rows_of(i)],
+            d_send.at[c, i, by - 1],
+            d_recv.at[c, i, by - 1],
+            device(x, y, target, core),
+        )
+
     both = [(c, d) for c in range(2) for d in range(2)]
 
-    def open_chunk(j):
+    def load(j, start, count):
         for c in range(2):
 
             @pl.loop(0, 32)
             def _(n, c=c):
-                part[c, j, lax.div(n, 8), lax.rem(n, 8)] = run[c, marks[c, 8, j * 32 + n]]
-
-        for c, d in both:
-            pending["first", c, d, j] = launch(first(c, d, j))
-        for c, d in both:
-            pending["direct", c, d, j] = launch(second(c, d, j, 1 - d))
-
-    def relay_chunk(j):
-        for c, d in both:
-            pending["first", c, d, j].wait_recv()
+                part[c, j, lax.div(n, 8), lax.rem(n, 8), start : start + count] = run[
+                    c, marks[c, 8, j * 32 + n], start : start + count
+                ]
+
+    def send_first(i):
+        for c, d in both:
+            pending["first", c, d, i] = launch(first(c, d, i))
+
+    def send_direct(i):
+        for c, d in both:
+            pending["direct", c, d, i] = launch(second(c, d, i, 1 - d))
+
+    def relay_chunk(i):
+        j, start, count, _ = CHUNKS[i]
+        for c, d in both:
+            pending["first", c, d, i].wait_recv()
             spot = shift(rings[c], signs[d], 4)
-            part[c, j, spot, 4 * d : 4 * d + 4] += near[c, d, j]
-            pending["relay", c, d, j] = launch(second(c, d, j, d))
-
-    def close_chunk(j):
-        for c, d in both:
-            pending["direct", c, d, j].wait_recv()
-            pending["relay", c, d, j].wait_recv()
-        for c in range(2):
-            part[c, j, rings[c]] += full[c, 0, j] + full[c, 1, j]
-
-    def z_step(j, step):
+            part[c, j, spot, 4 * d : 4 * d + 4, start : start + count] += near[c, d, j, :, start : start + count]
+            pending["relay", c, d, i] = launch(second(c, d, i, d))
+
+    def close_chunk(i):
+        j, start, count, _ = CHUNKS[i]
+        for c, d in both:
+            pending["direct", c, d, i].wait_recv()
+            pending["relay", c, d, i].wait_recv()
+        span = slice(start, start + count)
+        for c in range(2):
+            part[c, j, rings[c], :, span] += full[c, 0, j, :, span] + full[c, 1, j, :, span]
+
+    def send_straight(i):
+        for by in (4, 3, 5, 2, 6, 1, 7):
+            for c in range(2):
+                pending["straight", c, i, by] = launch(straight(c, i, by))
+
+    def z_step(i, step):
+        j, start, count, _ = CHUNKS[i]
         for c, d in both:
             if step > 1:
-                pending["z", c, d, j, step - 1].wait_recv()
+                pending["z", c, d, i, step - 1].wait_recv()
                 target = shift(z, signs[d] * (5 - step), 8)
-                rows = pl.ds(32 * d, 32) if step == 2 else pl.ds(0, 64)
+                rows = slice(start, start + count)
+                if step == 2:
+                    rows = slice(start + d * count // 2, start + (d + 1) * count // 2)
                 part[c, j, rings[c], target, rows] += zbuf[c, d, j, step - 2, rows]
-            if step < 5:
-                pending["z", c, d, j, step] = launch(along_z(c, d, j, step))
-
-    def finish_chunk(j):
-        tiles = []
+            pending["z", c, d, i, step] = launch(along_z(c, d, i, step))
+
+    rows_done = [0] * 4
+
+    def complete(j, count):
+        rows_done[j] += count
+        if rows_done[j] == 64:
+            out[:, j * 128 : (j + 1) * 128] = done[j].T
+
+    def finish(i):
+        j, start, count, chained = CHUNKS[i]
+        span = slice(start, start + count)
+        for c in range(2):
+            if chained:
+                for d in range(2):
+                    pending["z", c, d, i, 4].wait_recv()
+                tile = part[c, j, rings[c], z, span] + zbuf[c, 0, j, 3, span] + zbuf[c, 1, j, 3, span]
+            else:
+                tile = part[c, j, rings[c], z, span]
+                for by in range(1, 8):
+                    pending["straight", c, i, by].wait_recv()
+                    tile += zall[c, by - 1, span]
+            done[j, c * 64 + start : c * 64 + start + count, :] = tile
+        complete(j, count)
+
+    def wide_z(s, step):
+        j, start, count = WIDE[s]
+        for c, d in both:
+            target = shift(z, signs[d] * (5 - step), 8)
+            low, size = (start + d * count // 2, count // 2) if step < 3 else (start, count)
+            if step > 1:
+                pending["wide", c, d, s, step - 1].wait_recv()
+                part[c, j, :, target, low : low + size] += wbuf[c, d, step - 2, :, low : low + size]
+            rows = pl.ds(low, size) if step == 1 else pl.ds(start, count)
+            pending["wide", c, d, s, step] = launch(
+                remote(
+                    part.at[c, j, :, target, rows],
+                    wbuf.at[c, d, step - 1, :, rows],
+                    w_send.at[c, d, s, step - 1],
+                    w_recv.at[c, d, s, step - 1],
+                    z_ends[d],
+                )
+            )
+
+    def wide_ring(s):
+        j, start, count = WIDE[s]
+        span = slice(start, start + count)
         for c in range(2):
             for d in range(2):
-                pending["z", c, d, j, 4].wait_recv()
-            tiles.append(part[c, j, rings[c], z] + zbuf[c, 0, j, 3] + zbuf[c, 1, j, 3])
-        out[:, j * 128 : (j + 1) * 128] = jnp.concatenate(tiles, axis=0).T
-
-    for tick in range(5):
-        if tick < 4:
-            open_chunk(tick)
-        if tick > 0:
-            z_step(tick - 1, 1)
-            z_step(tick - 1, 2)
-        if tick < 4:
-            relay_chunk(tick)
-        if tick > 0:
-            z_step(tick - 1, 3)
-            z_step(tick - 1, 4)
-            finish_chunk(tick - 1)
-        if tick < 4:
-            close_chunk(tick)
+                pending["wide", c, d, s, 4].wait_recv()
+            part[c, j, :, z, span] += wbuf[c, 0, 3, :, span] + wbuf[c, 1, 3, :, span]
+            for d in range(2):
+                half = pl.ds(start + d * count // 2, count // 2)
+                pending["half", c, d, s] = launch(
+                    remote(
+                        part.at[c, j, shift(rings[c], 2, 4), z, half],
+                        ring.at[0, c, d, half],
+                        r_send.at[c, d, s, 0],
+                        r_recv.at[c, d, s, 0],
+                        ends[c][d],
+                    )
+                )
+
+    def wide_relay(s):
+        j, start, count = WIDE[s]
+        rows = pl.ds(start, count)
+        for c, d in both:
+            pending["half", c, d, s].wait_recv()
+            low, spot = start + d * count // 2, shift(rings[c], signs[d], 4)
+            half = slice(low, low + count // 2)
+            part[c, j, spot, z, half] += ring[0, c, d, half]
+            pending["whole", c, d, s] = launch(
+                remote(
+                    part.at[c, j, spot, z, rows],
+                    ring.at[1, c, d, rows],
+                    r_send.at[c, d, s, 1],
+                    r_recv.at[c, d, s, 1],
+                    ends[c][d],
+                )
+            )
+
+    def wide_finish(s):
+        j, start, count = WIDE[s]
+        span = slice(start, start + count)
+        for c in range(2):
+            for d in range(2):
+                pending["whole", c, d, s].wait_recv()
+            done[j, c * 64 + start : c * 64 + start + count, :] = (
+                part[c, j, rings[c], z, span] + ring[1, c, 0, span] + ring[1, c, 1, span]
+            )
+        complete(j, count)
+
+    steps = {
+        "load": lambda i: load(*CHUNKS[i][:3]), "first": send_first, "direct": send_direct, "relay": relay_chunk,
+        "close": close_chunk, "z": z_step, "straight": send_straight, "finish": finish,
+        "wload": lambda i: load(*WIDE[i]), "wz": wide_z, "wring": wide_ring, "wrelay": wide_relay, "wfinish": wide_finish,
+    }
+    for step in ORDER:
+        steps[step[0]](*step[1:])
     for copy in started:
         copy.wait_send()
 
@@ -340,15 +461,25 @@
             pltpu.VMEM((2, 2, 4, 4, 64, 128), F32),
             pltpu.VMEM((2, 2, 4, 8, 64, 128), F32),
             pltpu.VMEM((2, 2, 4, 4, 64, 128), F32),
+            pltpu.VMEM((2, 7, 64, 128), F32),
+            pltpu.VMEM((4, 128, 128), F32),
+            pltpu.VMEM((2, 2, 4, 4, 64, 128), F32),
+            pltpu.VMEM((2, 2, 2, 64, 128), F32),
             dma((8,)),
             dma((2, 14)),
             dma((2, 14)),
             dma((2, 7)),
             dma((2, 7)),
-            dma((2, 2, 4, 3)),
-            dma((2, 2, 4, 3)),
-            dma((2, 2, 4, 4)),
-            dma((2, 2, 4, 4)),
+            dma((2, 2, len(CHUNKS), 3)),
+            dma((2, 2, len(CHUNKS), 3)),
+            dma((2, 2, len(CHUNKS), 4)),
+            dma((2, 2, len(CHUNKS), 4)),
+            dma((2, len(CHUNKS), 7)),
+            dma((2, len(CHUNKS), 7)),
+            dma((2, 2, len(WIDE), 4)),
+            dma((2, 2, len(WIDE), 4)),
+            dma((2, 2, len(WIDE), 2)),
+            dma((2, 2, len(WIDE), 2)),
         ],
         compiler_params=pltpu.CompilerParams(
             collective_id=0, has_side_effects=True, vmem_limit_bytes=60 << 20

time: 114 us -> 88.1 us (0.77)
  Pallas kernels: 110 us -> 84.1 us
    pallas_call x1, Pallas kernels: 110 us -> 84.1 us  [body(): pl.pallas_call(kernel, name='coarse', out_shape=jax.ShapeDtypeStruct((128...]
where the time goes in v3:
time: 88.1 us; the launch traced here: 88 us
  Pallas kernels  84.1 us (95%)
  local copies, waits for them, and re-layouts  3.88 us (4%)
    pallas_call x1, Pallas kernels, body(): pl.pallas_call(kernel, name='coarse', out_shape=jax.ShapeDtypeStruct((128...  84.1 us
    unnamed x4, local copies, waits for them, and re-layouts  3.03 us

profile of v3, /device:TPU:32, one launch (start us, length us, event | category | flops | bytes accessed | tf_op | source)
XLA Modules:
  0.0 88.0 jit_solution(10046079729864953904)
XLA Ops:
  0.0 0.8 copy.5
  0.8 0.1 broadcast_in_dim.4
  0.8 0.0 copy-start
  0.8 0.1 reshape.8
  0.9 0.6 copy-done
  1.5 0.1 reshape.9
  1.6 0.6 pad.4.id_hbm
  2.2 84.1 %coarse.1 = f32[128,512]{1,0:T(8,128)} custom-call(bf16[4,2,128,128]{3,2,1,0:T(8,128)(2,1)} %p_hbm.1, bf16[4,6,128,128]{3,2,1,0:T(8,128)(2,1)} %q_hbm.1, s32[8,128]{1,0:T(8,128)} %pad.4.id_hbm), custom_call_target="tpu_custom_call" | custom-call | tf_op jit(solution)/shard_map/coarse/pallas_call | solution.py:446
  86.3 1.7 %copy.7 = f32[128,512]{1,0:T(8,128)} copy(f32[128,512]{1,0:T(8,128)} %coarse.1) | data formatting | bytes 524288
  (2 shorter events, 0.0 us)
Async XLA Ops:
  0.8 0.7 copy-start

commit v4 on v3

v4 whole, which is shorter than its diff:
```python
import jax
import jax.numpy as jnp
from jax import lax
from jax.experimental import pallas as pl
from jax.experimental.pallas import tpu as pltpu
from jax.sharding import PartitionSpec as P

MESH = pl.DeviceIdType.MESH
BF16, F32 = jnp.bfloat16, jnp.float32
ANY = pl.BlockSpec(memory_space=pl.ANY)
VMEM = pl.BlockSpec(memory_space=pltpu.VMEM)
SMEM = pl.BlockSpec(memory_space=pltpu.SMEM)
RECORD = 640
LOAD = 48
NONE = 8 * LOAD
HALF = 32
BLOCKS = ((0, 256 + 6 * HALF), (256 + 6 * HALF, 6 * HALF))
CHUNKS = ((16, 16), (32, 16), (48, 16))
WIDE = ((0, 16),)
ORDER = (
    ("wload", 0), ("wz", 0, 1), ("mul", 0), ("load", 0), ("near", 0), ("first", 0), ("mul", 1), ("mul", 2),
    ("direct", 0), ("wz", 0, 2), ("mul", 3), ("mul", 4), ("far", 0), ("mul", 5), ("relay", 0), ("mul", 6),
    ("mul", 7), ("load", 1), ("first", 1), ("load", 2), ("direct", 1), ("wz", 0, 3), ("relay", 1), ("close", 0),
    ("first", 2), ("z", 0, 1), ("wz", 0, 4), ("direct", 2), ("z", 0, 2), ("close", 1), ("relay", 2), ("z", 1, 1),
    ("z", 0, 3), ("z", 1, 2), ("wring", 0), ("close", 2), ("z", 2, 1), ("z", 1, 3), ("z", 2, 2), ("z", 1, 4),
    ("z", 2, 3), ("z", 0, 4), ("wrelay", 0), ("finish", 1), ("z", 2, 4), ("finish", 0), ("wfinish", 0),
    ("finish", 2),
)


def place():
    row, col = lax.axis_index("row"), lax.axis_index("col")
    core, z = lax.rem(row, 2), lax.rem(lax.div(row, 2), 8)
    x = lax.div(row, 16) * 2 + lax.rem(col, 2)
    return x, lax.div(col, 2), z, core


def device(x, y, z, core):
    return (lax.div(x, 2) * 16 + z * 2 + core, y * 2 + lax.rem(x, 2))


def shift(v, by, n):
    return lax.rem(v + (by + n), n)


def remote(src, dst, send, recv, where):
    return pltpu.make_async_remote_copy(
        src_ref=src, dst_ref=dst, send_sem=send, recv_sem=recv, device_id=where, device_id_type=MESH
    )


def kernel(
    p_hbm, q_hbm, p_cols, q_cols, out,
    p_in, q_in, held, ids, table, marks, run, part, near, full, zbuf, done, wbuf, ring,
    in_sem, g_send, g_recv, id_send, id_recv, s_send, s_recv, z_send, z_recv, w_send, w_recv, r_send, r_recv,
):
    x, y, z, core = place()
    other = 1 - core
    gather_rings, reduce_rings = (y, x), (x, y)

    def along_y(pos, who):
        return device(x, pos, z, who)

    def along_x(pos, who):
        return device(pos, y, z, who)

    gather_member, reduce_member = (along_y, along_x), (along_x, along_y)
    z_ends = [device(x, y, shift(z, d, 8), core) for d in (1, -1)]
    others = [(by, flip) for by in range(4) for flip in range(2) if by or flip]

    inputs = []
    for f in range(4):
        inputs.append(pltpu.make_async_copy(q_hbm.at[f], q_in.at[f], in_sem.at[f]))
    inputs.append(pltpu.make_async_copy(p_hbm, p_in, in_sem.at[4]))
    for copy in inputs:
        copy.start()

    partners = [along_y(shift(y, by, 4), other if flip else core) for by, flip in others]
    partners += [along_x(shift(x, by, 4), other if flip else core) for by, flip in others if by]
    partners += z_ends
    barrier = pltpu.get_barrier_semaphore()
    for partner in partners:
        pl.semaphore_signal(barrier, inc=1, device_id=partner, device_id_type=MESH)

    started = []

    def launch(copy):
        copy.start()
        started.append(copy)
        return copy

    slot = {0: 0, 1: 2, 3: 4, 2: 6}
    lane = lax.broadcasted_iota(jnp.int32, (8, 128), 1)
    rows = cols = jnp.zeros((8, 128), jnp.int32)
    for f in range(4):
        for k in range(2):
            low = (f * 2 + k) * 6
            rows = jnp.where(jnp.logical_and(lane >= low, lane < low + 6), p_cols[k, f], rows)
        for l in range(6):
            cols = jnp.where(jnp.logical_or(lane == f * 12 + l, lane == f * 12 + 6 + l), q_cols[f, l], cols)
    numbers = jnp.where(lax.broadcasted_iota(jnp.int32, (8, 128), 0) == 0, rows, cols)
    for c in range(2):
        ids[c, 0] = numbers

    def send_numbers():
        for c in range(2):
            for n, (by, flip) in enumerate(others):
                who = gather_member[c](shift(gather_rings[c], by, 4), other if flip else core)
                launch(remote(ids.at[c, 0], ids.at[c, slot[by] + flip], id_send.at[c, n], id_recv.at[c, n], who))

    def stage_block(f):
        inputs[f].wait()
        for c in range(2):
            for k in range(2):
                held[c, 0, f, k * 128 : (k + 1) * 128, :] = p_in[f, k]
        for l in range(6):
            flipped = q_in[f, l].T
            for c in range(2):
                for phase in range(2):
                    low, row = 256 + (phase * 6 + l) * HALF, c * 64 + phase * HALF
                    held[c, 0, f, low : low + HALF, :] = flipped[row : row + HALF]

    def send(phase, c, i, h, source, target, by, flip=False):
        at, rows = pl.ds(h * 2, 2), pl.ds(*BLOCKS[phase])
        who = gather_member[c](shift(gather_rings[c], by, 4), other if flip else core)
        launch(
            remote(
                held.at[c, source, at, rows],
                held.at[c, target, at, rows],
                g_send.at[c, phase, i],
                g_recv.at[c, phase, i],
                who,
            )
        )

    def arrived(phase, c, i, h, target):
        ref = held.at[c, target, pl.ds(h * 2, 2), pl.ds(*BLOCKS[phase])]
        who = gather_member[c](gather_rings[c], other)
        remote(ref, ref, g_send.at[c, phase, i], g_recv.at[c, phase, i], who).wait_recv()

    def send_own(phase):
        for c in range(2):
            send(phase, c, 3, 1, 0, 4, -1)
            send(phase, c, 1, 1, 0, 2, 1)
            send(phase, c, 2, 0, 0, 4, -1)
            send(phase, c, 7, 1, 0, 1, 0, True)

    inputs[4].wait()
    for f in range(2):
        stage_block(f)
    pl.semaphore_wait(barrier, len(partners))
    send_numbers()
    for c in range(2):
        send(0, c, 0, 0, 0, 2, 1)
        send(0, c, 6, 0, 0, 1, 0, True)
    for f in range(2, 4):
        stage_block(f)
    send_own(0)

    for c in range(2):
        for n, (by, flip) in enumerate(others):
            ref = ids.at[c, slot[by] + flip]
            remote(ref, ref, id_send.at[c, n], id_recv.at[c, n], gather_member[c](gather_rings[c], other)).wait_recv()
    below = lax.broadcasted_iota(jnp.int32, (LOAD, 128), 0)
    beside = lax.broadcasted_iota(jnp.int32, (LOAD, 128), 1)
    for c in range(2):
        rows = jnp.concatenate([ids[c, t, 0:1, :] for t in range(8)], axis=0)
        cols = jnp.concatenate([ids[c, t, 1:2, :] for t in range(8)], axis=0)
        mine = jnp.logical_and((rows & 1) == core, lane < LOAD)
        tile_x, tile_z = rows >> 4, (rows >> 1) & 7
        stop_y, stop_x, j = cols >> 3, (cols >> 2) & 1, cols & 3
        if c == 0:
            mine = jnp.logical_and(mine, stop_y == y)
            target = (tile_x * 2 + stop_x) * 32 + tile_z * 4 + j
        else:
            mine = jnp.logical_and(mine, jnp.logical_and(tile_x == lax.div(x, 2), stop_x == lax.rem(x, 2)))
            target = stop_y * 32 + tile_z * 4 + j
        target = jnp.where(mine, target, -1)
        flat = jnp.where(mine, target, -2).T[0:LOAD]
        last = jnp.full((1, 128), -1, jnp.int32)
        for t in range(8):
            same = jnp.broadcast_to(flat[:, t : t + 1], (LOAD, 128)) == beside
            last = jnp.maximum(last, jnp.max(jnp.where(same, below + t * LOAD, -1), axis=0, keepdims=True))
            found = jnp.full((1, 128), -1, jnp.int32)
            mark = jnp.broadcast_to(target[t : t + 1], (LOAD, 128))
            for u in range(t + 1):
                same = jnp.broadcast_to(flat[:, u : u + 1], (LOAD, 128)) == mark
                if u == t:
                    same = jnp.logical_and(same, below < beside)
                found = jnp.maximum(found, jnp.max(jnp.where(same, below + u * LOAD, -1), axis=0, keepdims=True))
            table[c, t : t + 1, :] = jnp.where(found < 0, NONE, found)
        table[c, 8:9, :] = jnp.where(last < 0, NONE, last)
        table[c, 9:16, :] = jnp.zeros((7, 128), jnp.int32)
        run[c, NONE] = jnp.zeros((64, 128), F32)
    copy = pltpu.make_async_copy(table, marks, in_sem.at[5])
    copy.start()
    copy.wait()

    def multiply(phase, c, t):
        low, rows = 256 + phase * 6 * HALF, slice(phase * HALF, (phase + 1) * HALF)

        for f in range(4):
            pair = jnp.concatenate([held[c, t, f, 0:128, :], held[c, t, f, 128:256, :]], axis=1)
            product = jnp.dot(held[c, t, f, low : low + 6 * HALF, :], pair, preferred_element_type=F32)
            for k in range(2):
                sums = []
                for l in range(6):
                    before = run[c, marks[c, t, f * 12 + k * 6 + l], rows]
                    sums.append(product[l * HALF : (l + 1) * HALF, k * 128 : (k + 1) * 128] + before)
                for l in range(6):
                    run[c, t * LOAD + f * 12 + k * 6 + l, rows] = sums[l]

    lent = {1: ((6, 0), (7, 1)), 3: ((8, 0), (9, 1)), 5: ((10, 0), (11, 1)), 7: ((12, 0), (13, 1))}

    def products(phase, t):
        for c in range(2):
            for i, h in lent.get(t, ()):
                arrived(phase, c, i, h, t)
            multiply(phase, c, t)

    def pass_near(phase):
        for c in range(2):
            arrived(phase, c, 0, 0, 2)
            send(phase, c, 4, 0, 2, 6, 1)
            send(phase, c, 8, 0, 2, 3, 0, True)
            arrived(phase, c, 3, 1, 4)
            send(phase, c, 5, 1, 4, 6, -1)
            send(phase, c, 11, 1, 4, 5, 0, True)

    def lend_near(phase):
        for c in range(2):
            arrived(phase, c, 1, 1, 2)
            send(phase, c, 9, 1, 2, 3, 0, True)
            arrived(phase, c, 2, 0, 4)
            send(phase, c, 10, 0, 4, 5, 0, True)

    def lend_far(phase):
        for c in range(2):
            arrived(phase, c, 4, 0, 6)
            send(phase, c, 12, 0, 6, 7, 0, True)
            arrived(phase, c, 5, 1, 6)
            send(phase, c, 13, 1, 6, 7, 0, True)

    products(0, 0)
    products(0, 1)
    pass_near(0)
    for c in range(2):
        send(1, c, 0, 0, 0, 2, 1)
        send(1, c, 6, 0, 0, 1, 0, True)
    send_own(1)
    lend_near(0)
    products(0, 2)
    products(0, 3)
    products(0, 4)
    products(0, 5)
    lend_far(0)
    products(0, 6)
    pass_near(1)
    products(0, 7)

    rings, signs = reduce_rings, (1, -1)
    ends = [[reduce_member[c](shift(rings[c], d, 4), core) for d in signs] for c in range(2)]
    pending = {}

    both = [(c, d) for c in range(2) for d in range(2)]

    def load(start, count):
        rows = slice(start, start + count)
        for c in range(2):

            @pl.loop(0, 8)
            def _(n, c=c):
                for m in range(4):
                    for j in range(4):
                        part[c, m, n, j, rows] = run[c, marks[c, 8, m * 32 + n * 4 + j], rows]

    def send_first(i):
        rows = pl.ds(*CHUNKS[i])
        for c, d in both:
            pending["first", c, d, i] = launch(
                remote(
                    part.at[c, shift(rings[c], 2, 4), pl.ds(4 * d, 4), :, rows],
                    near.at[c, d, :, :, rows],
                    s_send.at[c, d, i, 0],
                    s_recv.at[c, d, i, 0],
                    ends[c][d],
                )
            )

    def send_second(c, d, i, half):
        at, rows = pl.ds(4 * half, 4), pl.ds(*CHUNKS[i])
        n = 2 if half == d else 1
        pending["second", c, d, i, n] = launch(
            remote(
                part.at[c, shift(rings[c], signs[d], 4), at, :, rows],
                full.at[c, d, at, :, rows],
                s_send.at[c, d, i, n],
                s_recv.at[c, d, i, n],
                ends[c][d],
            )
        )

    def send_direct(i):
        for c, d in both:
            send_second(c, d, i, 1 - d)

    def relay(i):
        start, count = CHUNKS[i]
        span = slice(start, start + count)
        for c, d in both:
            pending["first", c, d, i].wait_recv()
            part[c, shift(rings[c], signs[d], 4), 4 * d : 4 * d + 4, :, span] += near[c, d, :, :, span]
            send_second(c, d, i, d)

    def close(i):
        start, count = CHUNKS[i]
        span = slice(start, start + count)
        for c, d in both:
            pending["second", c, d, i, 1].wait_recv()
            pending["second", c, d, i, 2].wait_recv()
        for c in range(2):
            part[c, rings[c], :, :, span] += full[c, 0, :, :, span] + full[c, 1, :, :, span]

    def along_z(i, step):
        start, count = CHUNKS[i]
        for c, d in both:
            target = shift(z, signs[d] * (5 - step), 8)
            low, size = (start + d * count // 2, count // 2) if step < 3 else (start, count)
            if step > 1:
                pending["z", c, d, i, step - 1].wait_recv()
                part[c, rings[c], target, :, low : low + size] += zbuf[c, d, step - 2, :, low : low + size]
            rows = pl.ds(low, size) if step == 1 else pl.ds(start, count)
            pending["z", c, d, i, step] = launch(
                remote(
                    part.at[c, rings[c], target, :, rows],
                    zbuf.at[c, d, step - 1, :, rows],
                    z_send.at[c, d, i, step - 1],
                    z_recv.at[c, d, i, step - 1],
                    z_ends[d],
                )
            )

    def finish(i):
        start, count = CHUNKS[i]
        span = slice(start, start + count)
        for c in range(2):
            for d in range(2):
                pending["z", c, d, i, 4].wait_recv()
            done[:, c * 64 + start : c * 64 + start + count] = (
                part[c, rings[c], z, :, span] + zbuf[c, 0, 3, :, span] + zbuf[c, 1, 3, :, span]
            )

    def wide_z(s, step):
        start, count = WIDE[s]
        for c, d in both:
            target = shift(z, signs[d] * (5 - step), 8)
            low, size = (start + d * count // 2, count // 2) if step < 3 else (start, count)
            if step > 1:
                pending["wide", c, d, s, step - 1].wait_recv()
                part[c, :, target, :, low : low + size] += wbuf[c, d, step - 2, :, :, low : low + size]
            rows = pl.ds(low, size) if step == 1 else pl.ds(start, count)
            pending["wide", c, d, s, step] = launch(
                remote(
                    part.at[c, :, target, :, rows],
                    wbuf.at[c, d, step - 1, :, :, rows],
                    w_send.at[c, d, s, step - 1],
                    w_recv.at[c, d, s, step - 1],
                    z_ends[d],
                )
            )

    def wide_ring(s):
        start, count = WIDE[s]
        span = slice(start, start + count)
        for c in range(2):
            for d in range(2):
                pending["wide", c, d, s, 4].wait_recv()
            part[c, :, z, :, span] += wbuf[c, 0, 3, :, :, span] + wbuf[c, 1, 3, :, :, span]
            for d in range(2):
                half = pl.ds(start + d * count // 2, count // 2)
                pending["half", c, d, s] = launch(
                    remote(
                        part.at[c, shift(rings[c], 2, 4), z, :, half],
                        ring.at[0, c, d, :, half],
                        r_send.at[c, d, s, 0],
                        r_recv.at[c, d, s, 0],
                        ends[c][d],
                    )
                )

    def wide_relay(s):
        start, count = WIDE[s]
        rows = pl.ds(start, count)
        for c, d in both:
            pending["half", c, d, s].wait_recv()
            low, spot = start + d * count // 2, shift(rings[c], signs[d], 4)
            half = slice(low, low + count // 2)
            part[c, spot, z, :, half] += ring[0, c, d, :, half]
            pending["whole", c, d, s] = launch(
                remote(
                    part.at[c, spot, z, :, rows],
                    ring.at[1, c, d, :, rows],
                    r_send.at[c, d, s, 1],
                    r_recv.at[c, d, s, 1],
                    ends[c][d],
                )
            )

    def wide_finish(s):
        start, count = WIDE[s]
        span = slice(start, start + count)
        for c in range(2):
            for d in range(2):
                pending["whole", c, d, s].wait_recv()
            done[:, c * 64 + start : c * 64 + start + count] = (
                part[c, rings[c], z, :, span] + ring[1, c, 0, :, span] + ring[1, c, 1, :, span]
            )

    steps = {
        "load": lambda i: load(*CHUNKS[i]), "first": send_first, "direct": send_direct, "relay": relay,
        "close": close, "z": along_z, "finish": finish, "wload": lambda i: load(*WIDE[i]), "wz": wide_z,
        "wring": wide_ring, "wrelay": wide_relay, "wfinish": wide_finish, "mul": lambda t: products(1, t),
        "near": lambda i: lend_near(1), "far": lambda i: lend_far(1),
    }
    for step in ORDER:
        steps[step[0]](*step[1:])
    for j in range(4):
        out[:, j * 128 : (j + 1) * 128] = done[j].T
    for copy in started:
        copy.wait_send()


def body(p_tiles, p_cols, q_tiles, q_cols):
    dma = pltpu.SemaphoreType.DMA
    return pl.pallas_call(
        kernel,
        name="coarse",
        out_shape=jax.ShapeDtypeStruct((128, 512), F32),
        in_specs=[ANY, ANY, SMEM, SMEM],
        out_specs=VMEM,
        scratch_shapes=[
            pltpu.VMEM((4, 2, 128, 128), BF16),
            pltpu.VMEM((4, 6, 128, 128), BF16),
            pltpu.VMEM((2, 8, 4, RECORD, 128), BF16),
            pltpu.VMEM((2, 8, 8, 128), jnp.int32),
            pltpu.VMEM((2, 16, 128), jnp.int32),
            pltpu.SMEM((2, 16, 128), jnp.int32),
            pltpu.VMEM((2, NONE + 1, 64, 128), F32),
            pltpu.VMEM((2, 4, 8, 4, 64, 128), F32),
            pltpu.VMEM((2, 2, 4, 4, 64, 128), F32),
            pltpu.VMEM((2, 2, 8, 4, 64, 128), F32),
            pltpu.VMEM((2, 2, 4, 4, 64, 128), F32),
            pltpu.VMEM((4, 128, 128), F32),
            pltpu.VMEM((2, 2, 4, 4, 4, HALF, 128), F32),
            pltpu.VMEM((2, 2, 2, 4, HALF, 128), F32),
            dma((6,)),
            dma((2, 2, 14)),
            dma((2, 2, 14)),
            dma((2, 7)),
            dma((2, 7)),
            dma((2, 2, len(CHUNKS), 3)),
            dma((2, 2, len(CHUNKS), 3)),
            dma((2, 2, len(CHUNKS), 4)),
            dma((2, 2, len(CHUNKS), 4)),
            dma((2, 2, len(WIDE), 4)),
            dma((2, 2, len(WIDE), 4)),
            dma((2, 2, len(WIDE), 2)),
            dma((2, 2, len(WIDE), 2)),
        ],
        compiler_params=pltpu.CompilerParams(
            collective_id=0, has_side_effects=True, vmem_limit_bytes=60 << 20
        ),
    )(p_tiles, q_tiles, p_cols.T, q_cols)


def solution(mesh):
    placed = (
        P(("row", "col"), None, None, None),
        P(("row", "col"), None),
        P(("row", "col"), None, None, None),
        P(("row", "col"), None),
    )
    return jax.shard_map(
        body, mesh=mesh, in_specs=placed, out_specs=P("row", "col"), check_vma=False
    )
```

time: 88.1 us -> 79.4 us (0.901)
  Pallas kernels: 84.1 us -> 77.3 us
  local copies, waits for them, and re-layouts: 3.88 us -> 1.67 us
    pallas_call x1, Pallas kernels: 84.1 us -> 77.3 us  [body(): pl.pallas_call(kernel, name='coarse', out_shape=jax.ShapeDtypeStruct((128...]
    unnamed x4 -> x1, local copies, waits for them, and re-layouts: 3.03 us -> 1.67 us
where the time goes in v4:
time: 79.4 us; the launch traced here: 79 us
  Pallas kernels  77.3 us (97%)
  local copies, waits for them, and re-layouts  1.67 us (2%)
    pallas_call x1, Pallas kernels, body(): pl.pallas_call(kernel, name='coarse', out_shape=jax.ShapeDtypeStruct((128...  77.3 us
    unnamed x1, local copies, waits for them, and re-layouts  1.67 us

profile of v4, /device:TPU:32, one launch (start us, length us, event | category | flops | bytes accessed | tf_op | source)
XLA Modules:
  0.0 79.0 jit_solution(5857936850670410110)
XLA Ops:
  0.0 77.3 %coarse.1 = f32[128,512]{1,0:T(8,128)} custom-call(bf16[4,2,128,128]{3,2,1,0:T(8,128)(2,1)} %p_hbm.1, bf16[4,6,128,128]{3,2,1,0:T(8,128)(2,1)} %q_hbm.1, s32[2,4]{1,0:T(2,128)} %bitcast.1, s32[4,6]{1,0:T(4,128)} %q_cols.1), custom_call_target="tpu_custom_call" | custom-call | tf_op jit(solution)/shard_map/coarse/pallas_call | solution.py:435
  77.3 1.7 %copy.6 = f32[128,512]{1,0:T(8,128)} copy(f32[128,512]{1,0:T(8,128)} %coarse.1) | data formatting | bytes 524288

commit v5 on v4

--- a/solution.py
+++ b/solution.py
@@ -267,10 +267,8 @@
     def load(start, count):
         rows = slice(start, start + count)
         for c in range(2):
-
-            @pl.loop(0, 8)
-            def _(n, c=c):
-                for m in range(4):
+            for m in range(4):
+                for n in range(8):
                     for j in range(4):
                         part[c, m, n, j, rows] = run[c, marks[c, 8, m * 32 + n * 4 + j], rows]
 

time: 79.4 us -> 78.7 us (level)
  no operation moved by 1% of the time
where the time goes in v5:
time: 78.7 us; the launch traced here: 78.2 us
  Pallas kernels  76.6 us (97%)
  local copies, waits for them, and re-layouts  1.67 us (2%)
    pallas_call x1, Pallas kernels, body(): pl.pallas_call(kernel, name='coarse', out_shape=jax.ShapeDtypeStruct((128...  76.6 us
    unnamed x1, local copies, waits for them, and re-layouts  1.67 us

profile of v5, /device:TPU:32, one launch (start us, length us, event | category | flops | bytes accessed | tf_op | source)
XLA Modules:
  0.0 78.2 jit_solution(10075445432872233799)
XLA Ops:
  0.0 76.6 %coarse.1 = f32[128,512]{1,0:T(8,128)} custom-call(bf16[4,2,128,128]{3,2,1,0:T(8,128)(2,1)} %p_hbm.1, bf16[4,6,128,128]{3,2,1,0:T(8,128)(2,1)} %q_hbm.1, s32[2,4]{1,0:T(2,128)} %bitcast.1, s32[4,6]{1,0:T(4,128)} %q_cols.1), custom_call_target="tpu_custom_call" | custom-call | tf_op jit(solution)/shard_map/coarse/pallas_call | solution.py:433
  76.6 1.7 %copy.6 = f32[128,512]{1,0:T(8,128)} copy(f32[128,512]{1,0:T(8,128)} %coarse.1) | data formatting | bytes 524288
